TPU v7x, 256 devices: a whole 4x4x8 slice. The times are simulated.
256 devices in a mesh: dp: 32 (over z, y_hi, core), fsdp: 8 (over y_lo, x).
Axes of the slice: x: 4, y: 4 (y_hi: 2, y_lo: 2; y = y_hi * 2 + y_lo), z: 8, core: 2. Of those that a mesh axis runs over, the one named last changes fastest.
Arguments:
- hidden: bfloat16 [131072, 1152], P(('dp', 'fsdp')), may hold values from -6 to 6
- text_ids: int32 [8192, 16], P(('dp', 'fsdp')), may hold values from 0 to 31999, as said below
- ln_gain: float32 [1152], replicated, may hold values from 0.5 to 1.5
- ln_bias: float32 [1152], replicated, may hold values from -2 to 2
- fc1_weight: bfloat16 [1152, 4304], P(None, 'fsdp'), may hold values from -0.1875 to 0.1875
- fc1_bias: float32 [4304], replicated, may hold values from -3 to 3
- fc2_weight: bfloat16 [4304, 1152], P('fsdp'), may hold values from -0.09375 to 0.09375
- fc2_bias: float32 [1152], replicated, may hold values from -3 to 3
- final_gain: float32 [1152], replicated, may hold values from 0.5 to 1.5
- final_bias: float32 [1152], replicated, may hold values from -0.2 to 0.2
- head_weight: bfloat16 [1152, 1152], replicated, may hold values from -0.1875 to 0.1875
- head_bias: float32 [1152], replicated, may hold values from -0.3 to 0.3
- image_emb: bfloat16 [8192, 1152], P(('dp', 'fsdp')), may hold values from -6 to 6
- teacher_logits: bfloat16 [8192, 12, 256], P('dp', None, 'fsdp'), may hold values from -12 to 12
- logit_scale: float32 [1], replicated, may hold values from 4 to 16
- logit_bias: float32 [1], replicated, may hold values from -3 to 0
Outputs:
- image_grad: float32 [8192, 1152], P(('dp', 'fsdp'))
Inputs may be any that keep to these rules, and one draw needn't show every extreme that they name: `text_ids`: 0 marks padding after a text's end; every text has at least one token and the tokens of a text come first.
All inputs are finite; a program needn't handle non-finite values.
Results may differ from a plain program's by a relative error of at most 0.0018.
Values may be sent and summed in bfloat16 or wider, within the bound.
No kernel may reach another device: no remote copies, remote signals or barrier semaphores. Data moves between devices by JAX's collectives and lax.ppermute only.
A program may use at most 128 MiB of HBM per device.

v0:
```python
import functools

import jax
import jax.numpy as jnp
from jax import lax
from jax.experimental import pallas as pl
from jax.experimental.pallas import tpu as pltpu
from jax.sharding import PartitionSpec as P


AXES = ("dp", "fsdp")
DEVICES = 256
PART = 136
TILE = 256


def place_of(device):
    dp, fs = divmod(device, 8)
    return fs % 4, ((dp >> 1) & 1) * 2 + (fs >> 2), dp >> 2, dp & 1


def device_at(x, y, z, c):
    x, y, z = x % 4, y % 4, z % 8
    return (z * 4 + (y >> 1) * 2 + c) * 8 + (y & 1) * 4 + x


def come_from(array, dx=0, dy=0, dz=0, dc=0):
    pairs = []
    for target in range(DEVICES):
        x, y, z, c = place_of(target)
        pairs.append((device_at(x + dx, y + dy, z + dz, c ^ dc), target))
    return lax.ppermute(array, AXES, pairs)


def here():
    dp, fs = lax.axis_index("dp"), lax.axis_index("fsdp")
    return fs % 4, ((dp // 2) % 2) * 2 + fs // 4, dp // 4, dp % 2


def normalise(values, gain, shift):
    centre = jnp.mean(values, axis=-1, keepdims=True)
    spread = jnp.mean((values - centre) ** 2, axis=-1, keepdims=True)
    return (values - centre) * lax.rsqrt(spread + 1e-06) * gain + shift


BLOCK = 128
ROWS_STEP = 256


def over_blocks(tokens, body):
    def step(i, carry):
        body(pl.ds(pl.multiple_of(i * BLOCK, BLOCK), BLOCK), i)
        return carry

    lax.fori_loop(0, tokens // BLOCK, step, 0)


def norm_kernel(hidden, gain, shift, normed):
    def body(rows, _):
        normed[rows] = normalise(
            hidden[rows].astype(jnp.float32), gain[...].reshape(1, -1), shift[...].reshape(1, -1)
        ).astype(jnp.bfloat16)

    over_blocks(hidden.shape[0], body)


def hidden_units(normed, up, bias):
    pre = (
        lax.dot_general(normed, up, (((1,), (1,)), ((), ())), preferred_element_type=jnp.float32)
        + bias
    )
    return jax.nn.gelu(pre, approximate=True).astype(jnp.bfloat16)


def cut(first, last, more=()):
    cuts = {first, last, *more} | {u for u in range(first, last) if u % PART == 0}
    cuts = sorted(cuts)
    return [(lo // PART, lo % PART, hi - lo, lo - first) for lo, hi in zip(cuts, cuts[1:])]


def assemble(first, last, parts, up, down):
    skipped = first // PART
    for part, row, rows, unit in cut(first, last):
        ref = parts[part - skipped]
        up[pl.ds(unit, rows)] = ref[pl.ds(row, rows)]
        down[pl.ds(unit, rows)] = ref[pl.ds(PART + row, rows)]


def bias_kernel(shard, places, flat, tiles, line, quarters):
    x, y, z, c = here()
    line[...] = flat[...].reshape(1, -1)
    quarters[...] = jnp.zeros(quarters.shape, quarters.dtype)
    for s in range(flat.shape[0] // shard):
        for q in range(4):
            size = min(PART, shard - q * PART)
            quarters[pl.ds(4 * s + q, 1), pl.ds(0, size)] = line[
                :, pl.ds(s * shard + q * PART, size)
            ]
    tiles[...] = jnp.zeros(tiles.shape, tiles.dtype)
    for part, row, rows, unit in cut(0, len(places) * PART, range(0, len(places) * PART, TILE)):
        dx, dy, other = places[part]
        place = (((y + dy) % 2) * 4 + (x + dx + 4) % 4) * 4 + 2 * c + (z + other) % 2
        values = quarters[pl.ds(place, 1), :]
        tiles[pl.ds(unit // TILE, 1), pl.ds(unit % TILE, rows)] = values[:, row : row + rows]


def part_kernel(ups, downs, *refs):
    outs, sems = refs[:2], refs[2]
    _, _, z, c = here()
    size = ups.shape[0]
    full, rest = (size - 3 * PART) // 8 * 8, (size - 3 * PART) % 8
    for k, out in enumerate(outs):
        quarter = 2 * c + (z + k) % 2

        @pl.when(quarter < 3)
        def _(k=k, out=out, quarter=quarter):
            for side, weight in enumerate((ups, downs)):
                rows = pl.ds(pl.multiple_of(quarter * PART, 8), PART)
                pltpu.make_async_copy(
                    weight.at[rows], out.at[pl.ds(side * PART, PART)], sems.at[k, side]
                ).start()
            for side, weight in enumerate((ups, downs)):
                pltpu.make_async_copy(
                    weight.at[pl.ds(0, PART)], out.at[pl.ds(side * PART, PART)], sems.at[k, side]
                ).wait()

        @pl.when(quarter == 3)
        def _(k=k, out=out):
            copies = []
            for side, weight in enumerate((ups, downs)):
                last = side * PART + full
                out[pl.ds(last, PART - full)] = jnp.zeros((PART - full, out.shape[1]), out.dtype)
                for j, (row, count) in enumerate(((0, full), (full, rest))):
                    copies.append(
                        pltpu.make_async_copy(
                            weight.at[pl.ds(3 * PART + row, count)],
                            out.at[pl.ds(side * PART + row, count)],
                            sems.at[k, 2 + 2 * side + j],
                        )
                    )
            for copy in copies:
                copy.start()
            for copy in copies:
                copy.wait()


def add_kernel(first, last, fresh, count, *refs):
    normed, bias = refs[:2], refs[2]
    before, rest = (refs[3:4], refs[4:]) if fresh else (refs[3:5], refs[5:])
    parts, totals = rest[:count], rest[count : count + 2]
    up, down = rest[-2:]
    if fresh:
        rest[count + 2][...] = (before[0][...] != 0).astype(jnp.float32)
    assemble(first, last, parts, up, down)
    blocks = normed[0].shape[0] // ROWS_STEP

    def step(tile, source):
        units = pl.ds(pl.multiple_of(tile * TILE, TILE), TILE)

        def rows_step(i, carry):
            rows = pl.ds(pl.multiple_of(i * ROWS_STEP, ROWS_STEP), ROWS_STEP)
            for k in range(2):
                act = hidden_units(normed[k][rows], up[units], bias[pl.ds(first // TILE + tile, 1)])
                term = jnp.dot(act, down[units], preferred_element_type=jnp.float32)
                totals[k][rows] = term if source is None else source[k][rows] + term
            return carry

        lax.fori_loop(0, blocks, rows_step, 0)

    def loop_step(tile, carry):
        step(tile, totals)
        return carry

    if fresh:
        step(0, None)
    else:
        lax.fori_loop(0, (last - first) // TILE, loop_step, 0)


def add_tiles(first, last, normed, bias, total, up, down):
    blocks = normed.shape[0] // ROWS_STEP
    steps = (last - first) // TILE
    rest = last - first - steps * TILE

    def rows_step(i, carry):
        rows = pl.ds(pl.multiple_of(i * ROWS_STEP, ROWS_STEP), ROWS_STEP)
        for tile in range(steps + (rest > 0)):
            size = TILE if tile < steps else rest
            units = pl.ds(tile * TILE, size)
            act = hidden_units(normed[rows], up[units], bias[pl.ds(first // TILE + tile, 1)][:, :size])
            total[rows] += jnp.dot(act, down[units], preferred_element_type=jnp.float32)
        return carry

    lax.fori_loop(0, blocks, rows_step, 0)


def finish_other_kernel(first, last, count, *refs):
    normed, bias, _ = refs[:3]
    parts = refs[3 : 3 + count]
    total, up, down = refs[3 + count :]
    assemble(first, last, parts, up, down)
    add_tiles(first, last, normed, bias, total, up, down)


def finish_own_kernel(first, last, normed, bias, before, up, down, hidden, fc2_bias, total):
    def body(rows, _):
        total[rows] = before[rows] + hidden[rows].astype(jnp.float32) + fc2_bias[...].reshape(1, -1)

    over_blocks(before.shape[0], body)
    add_tiles(first, last, normed, bias, total, up, down)


def unit_kernel(here_part, there_part, gain, shift, mask, head, head_bias, unit, pooled):
    width = unit.shape[1]
    seq = here_part.shape[0] // unit.shape[0]
    texts = BLOCK // seq

    def body(rows, i):
        out = here_part[rows] + there_part[rows]
        final = normalise(out, gain[...].reshape(1, -1), shift[...].reshape(1, -1))
        block = pl.ds(pl.multiple_of(i * texts, texts), texts)
        keep = mask[block]
        spread = jnp.broadcast_to(keep[:, None, :], (texts, seq, seq)).reshape(texts * seq, seq)
        at_row = lax.broadcasted_iota(jnp.int32, spread.shape, 0) % seq
        at_lane = lax.broadcasted_iota(jnp.int32, spread.shape, 1)
        kept = jnp.sum(jnp.where(at_row == at_lane, spread, 0.0), axis=1, keepdims=True)
        summed = jnp.sum((final * kept).reshape(texts, seq, width), axis=1)
        pooled[block] = summed / jnp.sum(keep, axis=1, keepdims=True)

    over_blocks(here_part.shape[0], body)
    emb = jnp.dot(
        pooled[...].astype(jnp.bfloat16), head[...], preferred_element_type=jnp.float32
    ) + head_bias[...].reshape(1, -1)
    unit[...] = (emb * lax.rsqrt(jnp.sum(emb * emb, axis=-1, keepdims=True) + 1e-06)).astype(
        jnp.bfloat16
    )


NEAR = (0, 1, 2, -1)
ROWS = tuple((dy, dc) for dc in (0, 1) for dy in NEAR)
TILES = ((0, 0), (2, 0), (1, 0), (2, 4))


def tile_kernel(tiles, own, near, far):
    x, y, _, c = here()
    column = (y // 2) * 2 + c
    _, group = tiles.shape[1:]
    half = group // 2
    for m, (target, at) in enumerate(((own, 0), (near, 0), (far, 0), (far, 4))):
        other = (column // 2 + m // 2) % 2 * 2 + (column % 2 + m % 2) % 2
        for d in range(4):
            step = jnp.clip(4 * d + other - column, 0, tiles.shape[0] - 1)
            tile = tiles[step].astype(jnp.float32)
            parts = [
                pltpu.roll(tile[:, k * half : (k + 1) * half], (4 - x) % 4 * (half // 4), 1)
                for k in range(2)
            ]
            target[at + d] = jnp.concatenate(parts, axis=1).astype(tiles.dtype)


def pack_kernel(near, far, both):
    both[:4] = near[...]
    both[4:] = far[4:]


def score_kernel(logit_scale, logit_bias, *refs):
    lines, images, tiles = refs[:8], refs[8:12], refs[12:15]
    grads, pictures, targets = refs[15:19], refs[19], refs[20]
    _, y, _, c = here()
    column = (y // 2) * 2 + c
    size, width = images[0].shape
    count = lines[0].shape[0]
    for d in range(4):
        pictures[pl.ds(d * size, size)] = images[d][...]
    for m in range(4):
        source, at = TILES[m]
        tile = tiles[source][at : at + 4].reshape(4 * size, 2 * count)
        for k in range(2):
            targets[m, k] = tile[:, k * count : (k + 1) * count]
    scale, offset = logit_scale[0], logit_bias[0]
    pics = pictures[...]
    total = jnp.zeros((4 * size, width), jnp.float32)
    far = lax.broadcasted_iota(jnp.int32, (4 * size, count), 0) // size
    for r, (dy, dc) in enumerate(ROWS):
        there = (y + dy + 4) % 4
        block = (there // 2) * 2 + (c + dc) % 2
        m = (there // 2 + y // 2) % 2 * 2 + dc
        units = lines[r][...]
        score = (
            scale
            * lax.dot_general(
                pics, units, (((1,), (1,)), ((), ())), preferred_element_type=jnp.float32
            )
            + offset
        )
        target = targets[m, there % 2].astype(jnp.float32)
        step = 4 * far + (column - block)
        weight = jnp.where(
            (step >= 0) & (step < 12), jax.nn.sigmoid(score) - jax.nn.sigmoid(target), 0.0
        ).astype(jnp.bfloat16)
        total = total + jnp.dot(weight, units, preferred_element_type=jnp.float32)
    for d in range(4):
        grads[d][...] = total[d * size : (d + 1) * size].astype(grads[d].dtype)


VMEM = pl.BlockSpec(memory_space=pltpu.VMEM)
ANY = pl.BlockSpec(memory_space=pl.ANY)
SMEM = pl.BlockSpec(memory_space=pltpu.SMEM)


def kernel_of(body, mib=10):
    return functools.partial(
        pl.pallas_call, body, compiler_params=pltpu.CompilerParams(vmem_limit_bytes=mib << 20)
    )


def in_hbm(array):
    return pltpu.with_memory_space_constraint(array, pltpu.HBM)


def after(values, *others):
    return lax.optimization_barrier((values, others))[0]


def on_device(
    hidden,
    text_ids,
    ln_gain,
    ln_bias,
    fc1_weight,
    fc1_bias,
    fc2_weight,
    fc2_bias,
    final_gain,
    final_bias,
    head_weight,
    head_bias,
    image_emb,
    teacher_logits,
    logit_scale,
    logit_bias,
):
    tokens, width = hidden.shape
    texts_here, _ = text_ids.shape
    hidden_here = fc1_weight.shape[1]

    part = pltpu.VMEM((2 * PART, width), jnp.bfloat16)
    own_p, own_q = kernel_of(part_kernel, 4)(
        out_shape=(part, part),
        in_specs=[pl.BlockSpec(memory_space=pltpu.HBM)] * 2,
        out_specs=(VMEM, VMEM),
        scratch_shapes=[pltpu.SemaphoreType.DMA((2, 6))],
        name="parts",
    )(in_hbm(fc1_weight.T), in_hbm(fc2_weight))
    right_p = come_from(own_p, dx=1)
    left_p = come_from(own_p, dx=-1)
    flip_p = come_from(own_p, dy=1)
    flip_q = come_from(own_q, dy=-1)

    places = (
        ((0, 0, 0), (0, 0, 1))
        + ((1, 0, 0), (-1, 0, 0), (0, 1, 0), (0, 1, 1))
        + ((1, 0, 1), (-1, 0, 1), (1, 1, 0), (-1, 1, 0), (2, 0, 0), (-1, 1, 1))
        + ((1, 1, 1), (2, 0, 1), (2, 1, 0), (2, 1, 1))
    )
    shards = fc1_bias.shape[0] // hidden_here
    units = len(places) * PART
    bias = kernel_of(functools.partial(bias_kernel, hidden_here, places), 4)(
        out_shape=pltpu.VMEM((-(-units // TILE), TILE), jnp.float32),
        in_specs=[VMEM],
        out_specs=VMEM,
        scratch_shapes=[
            pltpu.VMEM((1, fc1_bias.shape[0]), jnp.float32),
            pltpu.VMEM((4 * shards, TILE), jnp.float32),
        ],
        name="bias",
    )(fc1_bias)

    wide = pltpu.VMEM((tokens, width), jnp.float32)
    hidden = after(hidden, own_p)
    normed = kernel_of(norm_kernel, 4)(
        out_shape=pltpu.VMEM((tokens, width), jnp.bfloat16),
        in_specs=[VMEM] * 3,
        out_specs=VMEM,
        name="norm",
    )(hidden, ln_gain, ln_bias)
    normed = (normed, come_from(normed, dc=1))

    def scratch(first, last):
        return [pltpu.VMEM((last - first, width), jnp.bfloat16)] * 2

    def add_units(first, last, totals, parts):
        parts = parts[first // PART : -(-last // PART)]
        before = (text_ids,) if totals is None else totals
        keep = (pltpu.VMEM(text_ids.shape, jnp.float32),) if totals is None else ()
        return kernel_of(
            functools.partial(add_kernel, first, last, totals is None, len(parts))
        )(
            out_shape=(wide, wide) + keep,
            in_specs=[VMEM] * (3 + len(before) + len(parts)),
            out_specs=(VMEM,) * (2 + len(keep)),
            scratch_shapes=scratch(first, last),
            input_output_aliases={} if keep else {3: 0, 4: 1},
            name=f"units_{first}_{last}",
        )(*normed, bias, *before, *parts)

    parts = (own_p, own_q)
    *totals, keep = add_units(0, 256, None, parts)

    image_emb = after(image_emb, normed[0])
    images = image_emb.astype(jnp.float32)
    image_unit = (
        images * lax.rsqrt(jnp.sum(images * images, axis=-1, keepdims=True) + 1e-06)
    ).astype(jnp.bfloat16)
    pictures = [image_unit] + [come_from(image_unit, dz=d) for d in (1, 2, 3)]

    wave = after((right_p, left_p, flip_p, flip_q), totals, pictures)
    right_p, left_p, flip_p, flip_q = wave
    parts = parts + wave
    right_q = come_from(right_p, dz=1)
    left_q = come_from(left_p, dz=-1)
    flip_right_p = come_from(right_p, dy=1)
    flip_left_p = come_from(left_p, dy=-1)
    over_p = come_from(right_p, dx=1)
    flip_left_q = come_from(flip_q, dx=-1)
    totals = add_units(256, 768, totals, parts)

    teacher_logits = after(teacher_logits, wave)
    tiles = jnp.transpose(teacher_logits, (1, 2, 0))

    kinds = [pltpu.VMEM((n, *tiles.shape[1:]), tiles.dtype) for n in (4, 4, 8)]
    tiles_own, tiles_near, tiles_far = kernel_of(tile_kernel, 4)(
        out_shape=tuple(kinds), in_specs=[VMEM], out_specs=(VMEM,) * 3, name="tiles"
    )(tiles)
    tiles_far = come_from(tiles_far, dy=2)

    wave = after(
        (right_q, left_q, flip_right_p, flip_left_p, over_p, flip_left_q),
        totals,
        tiles_far,
    )
    right_q, left_q, flip_right_p, flip_left_p, over_p, flip_left_q = wave
    parts = parts + wave
    flip_right_q = come_from(flip_right_p, dz=1)
    over_q = come_from(over_p, dz=-1)
    flip_over_p = come_from(over_p, dy=1)
    flip_over_q = come_from(flip_left_q, dx=-1)
    tiles_swap = kernel_of(pack_kernel, 4)(
        out_shape=pltpu.VMEM(tiles_far.shape, tiles_far.dtype),
        in_specs=[VMEM] * 2,
        out_specs=VMEM,
        name="pack",
    )(tiles_near, after(tiles_far, wave))
    tile_sets = (tiles_own, tiles_far, come_from(tiles_swap, dc=1))
    totals = add_units(768, 1536, totals, parts)

    first, last = 1536, units
    parts = parts + after((flip_right_q, over_q, flip_over_p, flip_over_q), totals, tile_sets)
    parts = parts[first // PART :]

    rows = pltpu.VMEM((last - first, width), jnp.bfloat16)
    partial, up, down = kernel_of(
        functools.partial(finish_other_kernel, first, last, len(parts))
    )(
        out_shape=(wide, rows, rows),
        in_specs=[VMEM] * (3 + len(parts)),
        out_specs=(VMEM,) * 3,
        input_output_aliases={2: 0},
        name="finish_other",
    )(normed[1], bias, totals[1], *parts)
    there_part = come_from(partial, dc=1)
    here_part = kernel_of(functools.partial(finish_own_kernel, first, last))(
        out_shape=wide,
        in_specs=[VMEM] * 7,
        out_specs=VMEM,
        name="finish_own",
    )(normed[0], bias, totals[0], up, down, hidden, fc2_bias)
    text_unit = kernel_of(unit_kernel, 6)(
        out_shape=pltpu.VMEM((texts_here, width), jnp.bfloat16),
        in_specs=[VMEM] * 7,
        out_specs=VMEM,
        scratch_shapes=[pltpu.VMEM((texts_here, width), jnp.float32)],
        name="unit",
    )(here_part, there_part, final_gain, final_bias, keep, head_weight, head_bias)

    near_x = [text_unit] + [come_from(text_unit, dx=d) for d in NEAR[1:]]
    across = come_from(text_unit, dy=2)
    line = jnp.concatenate(near_x, axis=0)
    across = [across] + [come_from(across, dx=d) for d in NEAR[1:]]
    lines = [line, come_from(line, dy=1), jnp.concatenate(across, axis=0), come_from(line, dy=-1)]
    lines = lines + [come_from(part, dc=1) for part in lines]
    grads = kernel_of(score_kernel, 6)(
        out_shape=tuple(
            pltpu.VMEM((texts_here, width), kind)
            for kind in (jnp.float32, jnp.bfloat16, jnp.bfloat16, jnp.bfloat16)
        ),
        in_specs=[SMEM] * 2 + [VMEM] * 15,
        out_specs=(VMEM,) * 4,
        scratch_shapes=[
            pltpu.VMEM((4 * texts_here, width), jnp.bfloat16),
            pltpu.VMEM((4, 2, 4 * texts_here, 4 * texts_here), jnp.bfloat16),
        ],
        name="scores",
    )(logit_scale, logit_bias, *lines, *pictures, *tile_sets)
    total = grads[0]
    for d in (1, 2, 3):
        total = total + come_from(grads[d], dz=-d).astype(jnp.float32)
    return logit_scale[0] * total


def solution(mesh):
    placed = (
        P(("dp", "fsdp"), None),
        P(("dp", "fsdp"), None),
        P(),
        P(),
        P(None, "fsdp"),
        P(),
        P("fsdp", None),
        P(),
        P(),
        P(),
        P(),
        P(),
        P(("dp", "fsdp"), None),
        P("dp", None, "fsdp"),
        P(),
        P(),
    )
    return jax.shard_map(
        on_device, mesh=mesh, in_specs=placed, out_specs=P(("dp", "fsdp"), None), check_vma=False
    )
```

profile of v0, /device:TPU:1, one launch (start us, length us, event | category | flops | bytes accessed | tf_op | source)
XLA Modules:
  0.0 146.2 jit_solution(12292191008377133735)
XLA Ops:
  0.0 3.4 %parts.1 = (bf16[272,1152]{1,0:T(8,128)(2,1)}, bf16[272,1152]{1,0:T(8,128)(2,1)}) custom-call(bf16[538,1152]{1,0:T(8,128)(2,1)} %bitcast.5, bf16[538,1152]{1,0:T(8,128)(2,1)} %downs.1), custom_call_target="tpu_custom_call" | custom-call | tf_op jit(solution)/shard_map/parts/pallas_call | solution.py:348
  4.6 3.3 %collective-permute-start = (bf16[512,1152]{1,0:T(8,128)(2,1)S(1)}, bf16[512,1152]{1,0:T(8,128)(2,1)S(1)}, u32[]{:S(2)}, u32[]{:S(2)}) collective-permute-start(bf16[512,1152]{1,0:T(8,128)(2,1)S(1)} %norm.1.refs_0_.normed), channel_id=1, source_target_pairs={{8,0},{9,1},{10,2},{11,3},{12,4},{13,5},{14,6},{15,7},{0,8},{1,9},... | collective-permute-start | bytes 3538952 | tf_op jit(solution)/shard_map/ppermute | solution.py:32
  8.7 4.8 %collective-permute-start.7 = (bf16[32,1152]{1,0:T(8,128)(2,1)}, bf16[32,1152]{1,0:T(8,128)(2,1)S(1)}, u32[]{:S(2)}, u32[]{:S(2)}) collective-permute-start(bf16[32,1152]{1,0:T(8,128)(2,1)} %fusion.1.refs_8_), channel_id=1, source_target_pairs={{96,0},{97,1},{98,2},{99,3},{100,4},{101,5},{102,6},{103,7},{104,8... | collective-permute-start | bytes 221192 | tf_op jit(solution)/shard_map/ppermute | solution.py:32
  13.8 2.7 %collective-permute-start.3 = (bf16[272,1152]{1,0:T(8,128)(2,1)}, bf16[272,1152]{1,0:T(8,128)(2,1)}, u32[]{:S(2)}, u32[]{:S(2)}) collective-permute-start(bf16[272,1152]{1,0:T(8,128)(2,1)} %get-tuple-element.42.refs_4_), channel_id=1, source_target_pairs={{4,0},{5,1},{6,2},{7,3},{16,4},{17,5},{18,6},{19,7},{12,8},{13,9},... | collective-permute-start | bytes 1880072 | tf_op jit(solution)/shard_map/ppermute | solution.py:32
  19.1 2.5 %collective-permute-done.6.refs_10_ = bf16[32,1152]{1,0:T(8,128)(2,1)S(1)} collective-permute-done((bf16[32,1152]{1,0:T(8,128)(2,1)}, bf16[32,1152]{1,0:T(8,128)(2,1)S(1)}, u32[]{:S(2)}, u32[]{:S(2)}) %collective-permute-start.6) | collective-permute-done | bytes 73760 | tf_op jit(solution)/shard_map/ppermute | solution.py:32
  22.2 2.5 %collective-permute-start.1 = (bf16[272,1152]{1,0:T(8,128)(2,1)}, bf16[272,1152]{1,0:T(8,128)(2,1)}, u32[]{:S(2)}, u32[]{:S(2)}) collective-permute-start(bf16[272,1152]{1,0:T(8,128)(2,1)} %get-tuple-element.42.refs_4_), channel_id=1, source_target_pairs={{1,0},{2,1},{3,2},{0,3},{5,4},{6,5},{7,6},{4,7},{9,8},{10,9},{11,1... | collective-permute-start | bytes 1880072 | tf_op jit(solution)/shard_map/ppermute | solution.py:32
  28.8 4.8 %units_0_256.1 = (f32[512,1152]{1,0:T(8,128)S(1)}, f32[512,1152]{1,0:T(8,128)S(1)}, f32[32,16]{1,0:T(8,128)S(1)}) custom-call(bf16[512,1152]{1,0:T(8,128)(2,1)S(1)} %norm.1.refs_0_.normed, bf16[512,1152]{1,0:T(8,128)(2,1)S(1)} %collective-permute-done.refs_1_.refs_0_, f32[9,256]{1,0:T(8,128)S(1)} %bias.1.refs_2_.refs_1_, s32[32,16]{1,0:T(8,128)S(1)} %copy-done.7, ...), custom_call_target="tpu_custom_call" | custom-call | tf_op jit(solution)/shard_map/units_0_256/pallas_call | solution.py:396
  33.6 3.8 %collective-permute-done.1.refs_6_ = bf16[272,1152]{1,0:T(8,128)(2,1)} collective-permute-done((bf16[272,1152]{1,0:T(8,128)(2,1)}, bf16[272,1152]{1,0:T(8,128)(2,1)}, u32[]{:S(2)}, u32[]{:S(2)}) %collective-permute-start.1) | collective-permute-done | bytes 626720 | tf_op jit(solution)/shard_map/ppermute | solution.py:32
  38.9 2.7 %collective-permute-start.14 = (bf16[8,32,256]{2,1,0:T(8,128)(2,1)S(1)}, bf16[8,32,256]{2,1,0:T(8,128)(2,1)S(1)}, u32[]{:S(2)}, u32[]{:S(2)}) collective-permute-start(bf16[8,32,256]{2,1,0:T(8,128)(2,1)S(1)} %get-tuple-element.55), channel_id=1, source_target_pairs={{16,0},{17,1},{18,2},{19,3},{20,4},{21,5},{22,6},{23,7},{24,8},{25... | collective-permute-start | bytes 393224 | tf_op jit(solution)/shard_map/ppermute | solution.py:32
  42.3 2.7 %collective-permute-start.12 = (bf16[272,1152]{1,0:T(8,128)(2,1)}, bf16[272,1152]{1,0:T(8,128)(2,1)S(1)}, u32[]{:S(2)}, u32[]{:S(2)}) collective-permute-start(bf16[272,1152]{1,0:T(8,128)(2,1)} %collective-permute-done.1.refs_6_), channel_id=1, source_target_pairs={{1,0},{2,1},{3,2},{0,3},{5,4},{6,5},{7,6},{4,7},{9,8},{10,9},{11,1... | collective-permute-start | bytes 1880072 | tf_op jit(solution)/shard_map/ppermute | solution.py:32
  45.0 11.4 %collective-permute-done.14.far.refs_13_ = bf16[8,32,256]{2,1,0:T(8,128)(2,1)S(1)} collective-permute-done((bf16[8,32,256]{2,1,0:T(8,128)(2,1)S(1)}, bf16[8,32,256]{2,1,0:T(8,128)(2,1)S(1)}, u32[]{:S(2)}, u32[]{:S(2)}) %collective-permute-start.14) | collective-permute-done | bytes 131104 | tf_op jit(solution)/shard_map/ppermute | solution.py:32
  57.4 8.8 %units_256_768.1 = (f32[512,1152]{1,0:T(8,128)S(1)}, f32[512,1152]{1,0:T(8,128)S(1)}) custom-call(bf16[512,1152]{1,0:T(8,128)(2,1)S(1)} %norm.1.refs_0_.normed, bf16[512,1152]{1,0:T(8,128)(2,1)S(1)} %collective-permute-done.refs_1_.refs_0_, f32[9,256]{1,0:T(8,128)S(1)} %bias.1.refs_2_.refs_1_, ...), custom_call_target="tpu_custom_call", output_to_operand_aliasing={{0}: (3, {}), {1}: (4, {})} | custom-call | tf_op jit(solution)/shard_map/units_256_768/pallas_call | solution.py:396
  66.2 3.0 %collective-permute-done.10.refs_8_ = bf16[272,1152]{1,0:T(8,128)(2,1)S(1)} collective-permute-done((bf16[272,1152]{1,0:T(8,128)(2,1)}, bf16[272,1152]{1,0:T(8,128)(2,1)S(1)}, u32[]{:S(2)}, u32[]{:S(2)}) %collective-permute-start.10) | collective-permute-done | bytes 626720 | tf_op jit(solution)/shard_map/ppermute | solution.py:32
  69.3 3.1 %collective-permute-start.15 = (bf16[272,1152]{1,0:T(8,128)(2,1)S(1)}, bf16[272,1152]{1,0:T(8,128)(2,1)S(1)}, u32[]{:S(2)}, u32[]{:S(2)}) collective-permute-start(bf16[272,1152]{1,0:T(8,128)(2,1)S(1)} %collective-permute-done.10.refs_8_), channel_id=1, source_target_pairs={{32,0},{33,1},{34,2},{35,3},{36,4},{37,5},{38,6},{39,7},{40,8},{41... | collective-permute-start | bytes 1880072 | tf_op jit(solution)/shard_map/ppermute | solution.py:32
  73.5 5.0 %collective-permute-start.19 = (bf16[8,32,256]{2,1,0:T(8,128)(2,1)S(1)}, bf16[8,32,256]{2,1,0:T(8,128)(2,1)S(1)}, u32[]{:S(2)}, u32[]{:S(2)}) collective-permute-start(bf16[8,32,256]{2,1,0:T(8,128)(2,1)S(1)} %pack.1), channel_id=1, source_target_pairs={{8,0},{9,1},{10,2},{11,3},{12,4},{13,5},{14,6},{15,7},{0,8},{1,9},... | collective-permute-start | bytes 393224 | tf_op jit(solution)/shard_map/ppermute | solution.py:32
  78.6 11.5 %units_768_1536.1 = (f32[512,1152]{1,0:T(8,128)S(1)}, f32[512,1152]{1,0:T(8,128)S(1)}) custom-call(bf16[512,1152]{1,0:T(8,128)(2,1)S(1)} %norm.1.refs_0_.normed, bf16[512,1152]{1,0:T(8,128)(2,1)S(1)} %collective-permute-done.refs_1_.refs_0_, f32[9,256]{1,0:T(8,128)S(1)} %bias.1.refs_2_.refs_1_, ...), custom_call_target="tpu_custom_call", output_to_operand_aliasing={{0}: (3, {}), {1}: (4, {})} | custom-call | tf_op jit(solution)/shard_map/units_768_1536/pallas_call | solution.py:396
  90.1 4.2 %finish_other.1 = (f32[512,1152]{1,0:T(8,128)S(1)}, bf16[640,1152]{1,0:T(8,128)(2,1)S(1)}, bf16[640,1152]{1,0:T(8,128)(2,1)S(1)}) custom-call(bf16[512,1152]{1,0:T(8,128)(2,1)S(1)} %collective-permute-done.refs_1_.refs_0_, f32[9,256]{1,0:T(8,128)S(1)} %bias.1.refs_2_.refs_1_, ...), custom_call_target="tpu_custom_call", output_to_operand_aliasing={{0}: (2, {})} | custom-call | tf_op jit(solution)/shard_map/finish_other/pallas_call | solution.py:462
  95.9 4.2 %finish_own.1.here_part = f32[512,1152]{1,0:T(8,128)S(1)} custom-call(bf16[512,1152]{1,0:T(8,128)(2,1)S(1)} %norm.1.refs_0_.normed, f32[9,256]{1,0:T(8,128)S(1)} %bias.1.refs_2_.refs_1_, f32[512,1152]{1,0:T(8,128)S(1)} %get-tuple-element.62.before, bf16[640,1152]{1,0:T(8,128)(2,1)S(1)} %get-tuple-element.71.up, ...), custom_call_target="tpu_custom_call" | custom-call | tf_op jit(solution)/shard_map/finish_own/pallas_call | solution.py:472
  102.8 3.7 %collective-permute-start.22 = (bf16[32,1152]{1,0:T(8,128)(2,1)S(1)}, bf16[32,1152]{1,0:T(8,128)(2,1)S(1)}, u32[]{:S(2)}, u32[]{:S(2)}) collective-permute-start(bf16[32,1152]{1,0:T(8,128)(2,1)S(1)} %unit.1), channel_id=1, source_target_pairs={{2,0},{3,1},{0,2},{1,3},{6,4},{7,5},{4,6},{5,7},{10,8},{11,9},{8,1... | collective-permute-start | bytes 221192 | tf_op jit(solution)/shard_map/ppermute | solution.py:32
  107.4 3.2 %collective-permute-start.25 = (bf16[32,1152]{1,0:T(8,128)(2,1)S(1)}, bf16[32,1152]{1,0:T(8,128)(2,1)S(1)}, u32[]{:S(2)}, u32[]{:S(2)}) collective-permute-start(bf16[32,1152]{1,0:T(8,128)(2,1)S(1)} %unit.1), channel_id=1, source_target_pairs={{16,0},{17,1},{18,2},{19,3},{20,4},{21,5},{22,6},{23,7},{24,8},{25... | collective-permute-start | bytes 221192 | tf_op jit(solution)/shard_map/ppermute | solution.py:32
  123.6 3.0 %collective-permute-start.32 = (bf16[128,1152]{1,0:T(8,128)(2,1)S(1)}, bf16[128,1152]{1,0:T(8,128)(2,1)S(1)}, u32[]{:S(2)}, u32[]{:S(2)}) collective-permute-start(bf16[128,1152]{1,0:T(8,128)(2,1)S(1)} %constant_dynamic-update-slice_fusion.refs_2_), channel_id=1, source_target_pairs={{8,0},{9,1},{10,2},{11,3},{12,4},{13,5},{14,6},{15,7},{0,8},{1,9},... | collective-permute-start | bytes 884744 | tf_op jit(solution)/shard_map/ppermute | solution.py:32
  128.7 3.5 %scores.1 = (f32[32,1152]{1,0:T(8,128)S(1)}, bf16[32,1152]{1,0:T(8,128)(2,1)S(1)}, bf16[32,1152]{1,0:T(8,128)(2,1)S(1)}, bf16[32,1152]{1,0:T(8,128)(2,1)S(1)}) custom-call(f32[1]{0:T(128)} %copy.31.logit_scale, f32[1]{0:T(128)S(6)} %copy.32.logit_bias, bf16[128,1152]{1,0:T(8,128)(2,1)S(1)} %pad_maximum_fusion.refs_0_, ...), custom_call_target="tpu_custom_call" | custom-call | tf_op jit(solution)/shard_map/scores/pallas_call | solution.py:492
  133.4 4.7 %collective-permute-start.36 = (bf16[32,1152]{1,0:T(8,128)(2,1)S(1)}, bf16[32,1152]{1,0:T(8,128)(2,1)S(1)}, u32[]{:S(2)}, u32[]{:S(2)}) collective-permute-start(bf16[32,1152]{1,0:T(8,128)(2,1)S(1)} %get-tuple-element.78), channel_id=1, source_target_pairs={{160,0},{161,1},{162,2},{163,3},{164,4},{165,5},{166,6},{167,7},{1... | collective-permute-start | bytes 221192 | tf_op jit(solution)/shard_map/ppermute | solution.py:32
  140.1 5.4 %collective-permute-done.36 = bf16[32,1152]{1,0:T(8,128)(2,1)S(1)} collective-permute-done((bf16[32,1152]{1,0:T(8,128)(2,1)S(1)}, bf16[32,1152]{1,0:T(8,128)(2,1)S(1)}, u32[]{:S(2)}, u32[]{:S(2)}) %collective-permute-start.36) | collective-permute-done | bytes 73760 | tf_op jit(solution)/shard_map/ppermute | solution.py:32
  (104 shorter events, 36.6 us)
Async XLA Ops:
  4.6 20.1 %collective-permute-start = (bf16[512,1152]{1,0:T(8,128)(2,1)S(1)}, bf16[512,1152]{1,0:T(8,128)(2,1)S(1)}, u32[]{:S(2)}, u32[]{:S(2)}) collective-permute-start(bf16[512,1152]{1,0:T(8,128)(2,1)S(1)} %norm.1.refs_0_.normed), channel_id=1, source_target_pairs={{8,0},{9,1},{10,2},{11,3},{12,4},{13,5},{14,6},{15,7},{0,8},{1,9},... | collective-permute-start | bytes 3538952 | tf_op jit(solution)/shard_map/ppermute | solution.py:32
  8.7 8.5 %collective-permute-start.7 = (bf16[32,1152]{1,0:T(8,128)(2,1)}, bf16[32,1152]{1,0:T(8,128)(2,1)S(1)}, u32[]{:S(2)}, u32[]{:S(2)}) collective-permute-start(bf16[32,1152]{1,0:T(8,128)(2,1)} %fusion.1.refs_8_), channel_id=1, source_target_pairs={{96,0},{97,1},{98,2},{99,3},{100,4},{101,5},{102,6},{103,7},{104,8... | collective-permute-start | bytes 221192 | tf_op jit(solution)/shard_map/ppermute | solution.py:32
  13.8 19.8 %collective-permute-start.3 = (bf16[272,1152]{1,0:T(8,128)(2,1)}, bf16[272,1152]{1,0:T(8,128)(2,1)}, u32[]{:S(2)}, u32[]{:S(2)}) collective-permute-start(bf16[272,1152]{1,0:T(8,128)(2,1)} %get-tuple-element.42.refs_4_), channel_id=1, source_target_pairs={{4,0},{5,1},{6,2},{7,3},{16,4},{17,5},{18,6},{19,7},{12,8},{13,9},... | collective-permute-start | bytes 1880072 | tf_op jit(solution)/shard_map/ppermute | solution.py:32
  16.5 17.1 %collective-permute-start.4 = (bf16[272,1152]{1,0:T(8,128)(2,1)}, bf16[272,1152]{1,0:T(8,128)(2,1)}, u32[]{:S(2)}, u32[]{:S(2)}) collective-permute-start(bf16[272,1152]{1,0:T(8,128)(2,1)} %get-tuple-element.44.refs_5_), channel_id=1, source_target_pairs={{20,0},{21,1},{22,2},{23,3},{0,4},{1,5},{2,6},{3,7},{28,8},{29,9},... | collective-permute-start | bytes 1880072 | tf_op jit(solution)/shard_map/ppermute | solution.py:32
  17.9 15.8 %collective-permute-start.2 = (bf16[272,1152]{1,0:T(8,128)(2,1)}, bf16[272,1152]{1,0:T(8,128)(2,1)}, u32[]{:S(2)}, u32[]{:S(2)}) collective-permute-start(bf16[272,1152]{1,0:T(8,128)(2,1)} %get-tuple-element.42.refs_4_), channel_id=1, source_target_pairs={{3,0},{0,1},{1,2},{2,3},{7,4},{4,5},{5,6},{6,7},{11,8},{8,9},{9,10... | collective-permute-start | bytes 1880072 | tf_op jit(solution)/shard_map/ppermute | solution.py:32
  22.2 15.2 %collective-permute-start.1 = (bf16[272,1152]{1,0:T(8,128)(2,1)}, bf16[272,1152]{1,0:T(8,128)(2,1)}, u32[]{:S(2)}, u32[]{:S(2)}) collective-permute-start(bf16[272,1152]{1,0:T(8,128)(2,1)} %get-tuple-element.42.refs_4_), channel_id=1, source_target_pairs={{1,0},{2,1},{3,2},{0,3},{5,4},{6,5},{7,6},{4,7},{9,8},{10,9},{11,1... | collective-permute-start | bytes 1880072 | tf_op jit(solution)/shard_map/ppermute | solution.py:32
  24.7 8.9 %collective-permute-start.5 = (bf16[32,1152]{1,0:T(8,128)(2,1)}, bf16[32,1152]{1,0:T(8,128)(2,1)}, u32[]{:S(2)}, u32[]{:S(2)}) collective-permute-start(bf16[32,1152]{1,0:T(8,128)(2,1)} %fusion.1.refs_8_), channel_id=1, source_target_pairs={{32,0},{33,1},{34,2},{35,3},{36,4},{37,5},{38,6},{39,7},{40,8},{41... | collective-permute-start | bytes 221192 | tf_op jit(solution)/shard_map/ppermute | solution.py:32
  37.5 19.0 %collective-permute-start.11 = (bf16[272,1152]{1,0:T(8,128)(2,1)}, bf16[272,1152]{1,0:T(8,128)(2,1)S(1)}, u32[]{:S(2)}, u32[]{:S(2)}) collective-permute-start(bf16[272,1152]{1,0:T(8,128)(2,1)} %collective-permute-done.2.refs_7_), channel_id=1, source_target_pairs={{20,0},{21,1},{22,2},{23,3},{0,4},{1,5},{2,6},{3,7},{28,8},{29,9},... | collective-permute-start | bytes 1880072 | tf_op jit(solution)/shard_map/ppermute | solution.py:32
  38.9 17.5 %collective-permute-start.14 = (bf16[8,32,256]{2,1,0:T(8,128)(2,1)S(1)}, bf16[8,32,256]{2,1,0:T(8,128)(2,1)S(1)}, u32[]{:S(2)}, u32[]{:S(2)}) collective-permute-start(bf16[8,32,256]{2,1,0:T(8,128)(2,1)S(1)} %get-tuple-element.55), channel_id=1, source_target_pairs={{16,0},{17,1},{18,2},{19,3},{20,4},{21,5},{22,6},{23,7},{24,8},{25... | collective-permute-start | bytes 393224 | tf_op jit(solution)/shard_map/ppermute | solution.py:32
  41.6 24.6 %collective-permute-start.9 = (bf16[272,1152]{1,0:T(8,128)(2,1)}, bf16[272,1152]{1,0:T(8,128)(2,1)S(1)}, u32[]{:S(2)}, u32[]{:S(2)}) collective-permute-start(bf16[272,1152]{1,0:T(8,128)(2,1)} %collective-permute-done.2.refs_7_), channel_id=1, source_target_pairs={{224,0},{225,1},{226,2},{227,3},{228,4},{229,5},{230,6},{231,7},{2... | collective-permute-start | bytes 1880072 | tf_op jit(solution)/shard_map/ppermute | solution.py:32
  41.6 24.6 %collective-permute-start.13 = (bf16[272,1152]{1,0:T(8,128)(2,1)}, bf16[272,1152]{1,0:T(8,128)(2,1)S(1)}, u32[]{:S(2)}, u32[]{:S(2)}) collective-permute-start(bf16[272,1152]{1,0:T(8,128)(2,1)} %collective-permute-done.4.refs_9_.refs_5_), channel_id=1, source_target_pairs={{3,0},{0,1},{1,2},{2,3},{7,4},{4,5},{5,6},{6,7},{11,8},{8,9},{9,10... | collective-permute-start | bytes 1880072 | tf_op jit(solution)/shard_map/ppermute | solution.py:32
  42.3 23.9 %collective-permute-start.12 = (bf16[272,1152]{1,0:T(8,128)(2,1)}, bf16[272,1152]{1,0:T(8,128)(2,1)S(1)}, u32[]{:S(2)}, u32[]{:S(2)}) collective-permute-start(bf16[272,1152]{1,0:T(8,128)(2,1)} %collective-permute-done.1.refs_6_), channel_id=1, source_target_pairs={{1,0},{2,1},{3,2},{0,3},{5,4},{6,5},{7,6},{4,7},{9,8},{10,9},{11,1... | collective-permute-start | bytes 1880072 | tf_op jit(solution)/shard_map/ppermute | solution.py:32
  56.4 12.8 %collective-permute-start.10 = (bf16[272,1152]{1,0:T(8,128)(2,1)}, bf16[272,1152]{1,0:T(8,128)(2,1)S(1)}, u32[]{:S(2)}, u32[]{:S(2)}) collective-permute-start(bf16[272,1152]{1,0:T(8,128)(2,1)} %collective-permute-done.1.refs_6_), channel_id=1, source_target_pairs={{4,0},{5,1},{6,2},{7,3},{16,4},{17,5},{18,6},{19,7},{12,8},{13,9},... | collective-permute-start | bytes 1880072 | tf_op jit(solution)/shard_map/ppermute | solution.py:32
  56.4 12.8 %collective-permute-start.8 = (bf16[272,1152]{1,0:T(8,128)(2,1)}, bf16[272,1152]{1,0:T(8,128)(2,1)S(1)}, u32[]{:S(2)}, u32[]{:S(2)}) collective-permute-start(bf16[272,1152]{1,0:T(8,128)(2,1)} %collective-permute-done.1.refs_6_), channel_id=1, source_target_pairs={{32,0},{33,1},{34,2},{35,3},{36,4},{37,5},{38,6},{39,7},{40,8},{41... | collective-permute-start | bytes 1880072 | tf_op jit(solution)/shard_map/ppermute | solution.py:32
  69.3 20.8 %collective-permute-start.15 = (bf16[272,1152]{1,0:T(8,128)(2,1)S(1)}, bf16[272,1152]{1,0:T(8,128)(2,1)S(1)}, u32[]{:S(2)}, u32[]{:S(2)}) collective-permute-start(bf16[272,1152]{1,0:T(8,128)(2,1)S(1)} %collective-permute-done.10.refs_8_), channel_id=1, source_target_pairs={{32,0},{33,1},{34,2},{35,3},{36,4},{37,5},{38,6},{39,7},{40,8},{41... | collective-permute-start | bytes 1880072 | tf_op jit(solution)/shard_map/ppermute | solution.py:32
  72.3 17.8 %collective-permute-start.17 = (bf16[272,1152]{1,0:T(8,128)(2,1)S(1)}, bf16[272,1152]{1,0:T(8,128)(2,1)S(1)}, u32[]{:S(2)}, u32[]{:S(2)}) collective-permute-start(bf16[272,1152]{1,0:T(8,128)(2,1)S(1)} %collective-permute-done.12.refs_10_), channel_id=1, source_target_pairs={{4,0},{5,1},{6,2},{7,3},{16,4},{17,5},{18,6},{19,7},{12,8},{13,9},... | collective-permute-start | bytes 1880072 | tf_op jit(solution)/shard_map/ppermute | solution.py:32
  73.2 16.9 %collective-permute-start.16 = (bf16[272,1152]{1,0:T(8,128)(2,1)S(1)}, bf16[272,1152]{1,0:T(8,128)(2,1)S(1)}, u32[]{:S(2)}, u32[]{:S(2)}) collective-permute-start(bf16[272,1152]{1,0:T(8,128)(2,1)S(1)} %collective-permute-done.12.refs_10_), channel_id=1, source_target_pairs={{224,0},{225,1},{226,2},{227,3},{228,4},{229,5},{230,6},{231,7},{2... | collective-permute-start | bytes 1880072 | tf_op jit(solution)/shard_map/ppermute | solution.py:32
  73.2 17.0 %collective-permute-start.18 = (bf16[272,1152]{1,0:T(8,128)(2,1)S(1)}, bf16[272,1152]{1,0:T(8,128)(2,1)S(1)}, u32[]{:S(2)}, u32[]{:S(2)}) collective-permute-start(bf16[272,1152]{1,0:T(8,128)(2,1)S(1)} %collective-permute-done.13.refs_11_.refs_3_), channel_id=1, source_target_pairs={{3,0},{0,1},{1,2},{2,3},{7,4},{4,5},{5,6},{6,7},{11,8},{8,9},{9,10... | collective-permute-start | bytes 1880072 | tf_op jit(solution)/shard_map/ppermute | solution.py:32
  73.5 16.5 %collective-permute-start.19 = (bf16[8,32,256]{2,1,0:T(8,128)(2,1)S(1)}, bf16[8,32,256]{2,1,0:T(8,128)(2,1)S(1)}, u32[]{:S(2)}, u32[]{:S(2)}) collective-permute-start(bf16[8,32,256]{2,1,0:T(8,128)(2,1)S(1)} %pack.1), channel_id=1, source_target_pairs={{8,0},{9,1},{10,2},{11,3},{12,4},{13,5},{14,6},{15,7},{0,8},{1,9},... | collective-permute-start | bytes 393224 | tf_op jit(solution)/shard_map/ppermute | solution.py:32
  110.6 17.8 %collective-permute-start.30 = (bf16[128,1152]{1,0:T(8,128)(2,1)S(1)}, bf16[128,1152]{1,0:T(8,128)(2,1)S(1)}, u32[]{:S(2)}, u32[]{:S(2)}) collective-permute-start(bf16[128,1152]{1,0:T(8,128)(2,1)S(1)} %pad_maximum_fusion.refs_0_), channel_id=1, source_target_pairs={{8,0},{9,1},{10,2},{11,3},{12,4},{13,5},{14,6},{15,7},{0,8},{1,9},... | collective-permute-start | bytes 884744 | tf_op jit(solution)/shard_map/ppermute | solution.py:32
  112.1 14.5 %collective-permute-start.29 = (bf16[128,1152]{1,0:T(8,128)(2,1)S(1)}, bf16[128,1152]{1,0:T(8,128)(2,1)S(1)}, u32[]{:S(2)}, u32[]{:S(2)}) collective-permute-start(bf16[128,1152]{1,0:T(8,128)(2,1)S(1)} %pad_maximum_fusion.refs_0_), channel_id=1, source_target_pairs={{20,0},{21,1},{22,2},{23,3},{0,4},{1,5},{2,6},{3,7},{28,8},{29,9},... | collective-permute-start | bytes 884744 | tf_op jit(solution)/shard_map/ppermute | solution.py:32
  112.3 14.4 %collective-permute-start.24 = (bf16[128,1152]{1,0:T(8,128)(2,1)S(1)}, bf16[128,1152]{1,0:T(8,128)(2,1)S(1)}, u32[]{:S(2)}, u32[]{:S(2)}) collective-permute-start(bf16[128,1152]{1,0:T(8,128)(2,1)S(1)} %pad_maximum_fusion.refs_0_), channel_id=1, source_target_pairs={{4,0},{5,1},{6,2},{7,3},{16,4},{17,5},{18,6},{19,7},{12,8},{13,9},... | collective-permute-start | bytes 884744 | tf_op jit(solution)/shard_map/ppermute | solution.py:32
  114.7 8.8 %collective-permute-start.28 = (bf16[32,1152]{1,0:T(8,128)(2,1)S(1)}, bf16[32,1152]{1,0:T(8,128)(2,1)S(1)}, u32[]{:S(2)}, u32[]{:S(2)}) collective-permute-start(bf16[32,1152]{1,0:T(8,128)(2,1)S(1)} %collective-permute-done.25), channel_id=1, source_target_pairs={{3,0},{0,1},{1,2},{2,3},{7,4},{4,5},{5,6},{6,7},{11,8},{8,9},{9,10... | collective-permute-start | bytes 221192 | tf_op jit(solution)/shard_map/ppermute | solution.py:32
  133.4 12.1 %collective-permute-start.36 = (bf16[32,1152]{1,0:T(8,128)(2,1)S(1)}, bf16[32,1152]{1,0:T(8,128)(2,1)S(1)}, u32[]{:S(2)}, u32[]{:S(2)}) collective-permute-start(bf16[32,1152]{1,0:T(8,128)(2,1)S(1)} %get-tuple-element.78), channel_id=1, source_target_pairs={{160,0},{161,1},{162,2},{163,3},{164,4},{165,5},{166,6},{167,7},{1... | collective-permute-start | bytes 221192 | tf_op jit(solution)/shard_map/ppermute | solution.py:32
  (29 other events, 208.3 us)
where the time goes:
time: 148 us; the launch traced here: 146 us
  starting transfers between devices  62.6 us (42%)
  Pallas kernels  44.1 us (30%)
  waiting for transfers between devices  32.8 us (22%)
  local copies, waits for them, and re-layouts  3.45 us (2%)
  between operations  1.69 us (1%)
  other arithmetic  1.58 us (1%)
    ppermute x37, starting transfers between devices, come_from(): return lax.ppermute(array, AXES, pairs)  62.6 us
    ppermute x37, waiting for transfers between devices, come_from(): return lax.ppermute(array, AXES, pairs)  32.8 us
    pallas_call x3, Pallas kernels, add_units(): kernel_of(functools.partial(add_kernel, first, last, totals is None, len(...  25.1 us
    pallas_call x1, Pallas kernels, on_device(): kernel_of(functools.partial(finish_own_kernel, first, last))  4.23 us
    pallas_call x1, Pallas kernels, on_device(): kernel_of(functools.partial(finish_other_kernel, first, last, len(parts)))  4.15 us
    pallas_call x1, Pallas kernels, on_device(): kernel_of(score_kernel, 6)  3.53 us
    unnamed x36, local copies, waits for them, and re-layouts  3.44 us
    pallas_call x1, Pallas kernels, on_device(): kernel_of(part_kernel, 4)  3.4 us
  transfers between devices with their start and end apart: 37, of which 10 were waited for; matrix products, arithmetic and copies ran while one was open for 2% of the time, Pallas kernels for 20%

commit v1 on v0

--- a/solution.py
+++ b/solution.py
@@ -44,7 +44,8 @@
 
 
 BLOCK = 128
-ROWS_STEP = 256
+ROWS_STEP = 512
+SHORT_STEP = 256
 
 
 def over_blocks(tokens, body):
@@ -109,105 +110,116 @@
     _, _, z, c = here()
     size = ups.shape[0]
     full, rest = (size - 3 * PART) // 8 * 8, (size - 3 * PART) % 8
-    for k, out in enumerate(outs):
-        quarter = 2 * c + (z + k) % 2
-
-        @pl.when(quarter < 3)
-        def _(k=k, out=out, quarter=quarter):
-            for side, weight in enumerate((ups, downs)):
-                rows = pl.ds(pl.multiple_of(quarter * PART, 8), PART)
-                pltpu.make_async_copy(
-                    weight.at[rows], out.at[pl.ds(side * PART, PART)], sems.at[k, side]
-                ).start()
-            for side, weight in enumerate((ups, downs)):
-                pltpu.make_async_copy(
-                    weight.at[pl.ds(0, PART)], out.at[pl.ds(side * PART, PART)], sems.at[k, side]
-                ).wait()
-
-        @pl.when(quarter == 3)
-        def _(k=k, out=out):
-            copies = []
-            for side, weight in enumerate((ups, downs)):
-                last = side * PART + full
-                out[pl.ds(last, PART - full)] = jnp.zeros((PART - full, out.shape[1]), out.dtype)
-                for j, (row, count) in enumerate(((0, full), (full, rest))):
-                    copies.append(
-                        pltpu.make_async_copy(
-                            weight.at[pl.ds(3 * PART + row, count)],
-                            out.at[pl.ds(side * PART + row, count)],
-                            sems.at[k, 2 + 2 * side + j],
-                        )
-                    )
-            for copy in copies:
-                copy.start()
-            for copy in copies:
-                copy.wait()
-
-
-def add_kernel(first, last, fresh, count, *refs):
-    normed, bias = refs[:2], refs[2]
-    before, rest = (refs[3:4], refs[4:]) if fresh else (refs[3:5], refs[5:])
-    parts, totals = rest[:count], rest[count : count + 2]
-    up, down = rest[-2:]
-    if fresh:
-        rest[count + 2][...] = (before[0][...] != 0).astype(jnp.float32)
+
+    def whole(k, row):
+        return [
+            pltpu.make_async_copy(
+                weight.at[pl.ds(row, PART)], outs[k].at[pl.ds(side * PART, PART)], sems.at[k, side]
+            )
+            for side, weight in enumerate((ups, downs))
+        ]
+
+    def short(k):
+        return [
+            pltpu.make_async_copy(
+                weight.at[pl.ds(3 * PART + row, count)],
+                outs[k].at[pl.ds(side * PART + row, count)],
+                sems.at[k, 2 + 2 * side + j],
+            )
+            for side, weight in enumerate((ups, downs))
+            for j, (row, count) in enumerate(((0, full), (full, rest)))
+        ]
+
+    for waiting in (False, True):
+        for k, out in enumerate(outs):
+            quarter = 2 * c + (z + k) % 2
+
+            @pl.when(quarter < 3)
+            def _(k=k, quarter=quarter, waiting=waiting):
+                for copy in whole(k, pl.multiple_of(quarter * PART, 8)):
+                    copy.wait() if waiting else copy.start()
+
+            @pl.when(quarter == 3)
+            def _(k=k, out=out, waiting=waiting):
+                if not waiting:
+                    for side in range(2):
+                        zeros = jnp.zeros((PART - full, out.shape[1]), out.dtype)
+                        out[pl.ds(side * PART + full, PART - full)] = zeros
+                for copy in short(k):
+                    copy.wait() if waiting else copy.start()
+
+
+def add_term(first, tile, size, rows, normed, bias, up, down):
+    units = pl.ds(tile * TILE, size)
+    act = hidden_units(normed[rows], up[units], bias[pl.ds(first // TILE + tile, 1)][:, :size])
+    return jnp.dot(act, down[units], preferred_element_type=jnp.float32)
+
+
+def first_kernel(last, own, other, bias, ids, part_p, part_q, normed, total, mask, up, down):
+    mask[...] = (ids[...] != 0).astype(jnp.float32)
+    count = own.shape[0]
+    normed[:count] = own[...]
+    normed[count:] = other[...]
+    assemble(0, last, (part_p, part_q), up, down)
+
+    def step(i, carry):
+        rows = pl.ds(pl.multiple_of(i * SHORT_STEP, SHORT_STEP), SHORT_STEP)
+        total[rows] = add_term(0, 0, TILE, rows, normed, bias, up, down)
+        return carry
+
+    lax.fori_loop(0, normed.shape[0] // SHORT_STEP, step, 0)
+
+
+def add_kernel(first, last, count, normed, bias, _, *refs):
+    parts, (total, up, down) = refs[:count], refs[count:]
     assemble(first, last, parts, up, down)
-    blocks = normed[0].shape[0] // ROWS_STEP
-
-    def step(tile, source):
-        units = pl.ds(pl.multiple_of(tile * TILE, TILE), TILE)
-
-        def rows_step(i, carry):
-            rows = pl.ds(pl.multiple_of(i * ROWS_STEP, ROWS_STEP), ROWS_STEP)
-            for k in range(2):
-                act = hidden_units(normed[k][rows], up[units], bias[pl.ds(first // TILE + tile, 1)])
-                term = jnp.dot(act, down[units], preferred_element_type=jnp.float32)
-                totals[k][rows] = term if source is None else source[k][rows] + term
-            return carry
-
-        lax.fori_loop(0, blocks, rows_step, 0)
-
-    def loop_step(tile, carry):
-        step(tile, totals)
+    blocks = normed.shape[0] // ROWS_STEP
+
+    def step(i, carry):
+        rows = pl.ds(pl.multiple_of(i % blocks * ROWS_STEP, ROWS_STEP), ROWS_STEP)
+        total[rows] += add_term(first, i // blocks, TILE, rows, normed, bias, up, down)
         return carry
 
-    if fresh:
-        step(0, None)
-    else:
-        lax.fori_loop(0, (last - first) // TILE, loop_step, 0)
-
-
-def add_tiles(first, last, normed, bias, total, up, down):
-    blocks = normed.shape[0] // ROWS_STEP
+    lax.fori_loop(0, (last - first) // TILE * blocks, step, 0)
+
+
+def add_tiles(first, last, base, normed, bias, total, up, down):
     steps = (last - first) // TILE
     rest = last - first - steps * TILE
-
-    def rows_step(i, carry):
-        rows = pl.ds(pl.multiple_of(i * ROWS_STEP, ROWS_STEP), ROWS_STEP)
-        for tile in range(steps + (rest > 0)):
-            size = TILE if tile < steps else rest
-            units = pl.ds(tile * TILE, size)
-            act = hidden_units(normed[rows], up[units], bias[pl.ds(first // TILE + tile, 1)][:, :size])
-            total[rows] += jnp.dot(act, down[units], preferred_element_type=jnp.float32)
+    tokens = total.shape[0]
+
+    def step(tile, carry):
+        total[...] += add_term(first, tile, TILE, pl.ds(base, tokens), normed, bias, up, down)
         return carry
 
-    lax.fori_loop(0, blocks, rows_step, 0)
-
-
-def finish_other_kernel(first, last, count, *refs):
-    normed, bias, _ = refs[:3]
-    parts = refs[3 : 3 + count]
-    total, up, down = refs[3 + count :]
+    lax.fori_loop(0, steps, step, 0)
+
+    def rest_step(i, carry):
+        start = pl.multiple_of(i * SHORT_STEP, SHORT_STEP)
+        rows = pl.ds(base + start, SHORT_STEP)
+        total[pl.ds(start, SHORT_STEP)] += add_term(
+            first, steps, rest, rows, normed, bias, up, down
+        )
+        return carry
+
+    if rest:
+        lax.fori_loop(0, tokens // SHORT_STEP, rest_step, 0)
+
+
+def finish_other_kernel(first, last, count, normed, bias, before, *refs):
+    parts, (total, up, down) = refs[:count], refs[count:]
     assemble(first, last, parts, up, down)
-    add_tiles(first, last, normed, bias, total, up, down)
+    tokens = total.shape[0]
+    total[...] = before[tokens:]
+    add_tiles(first, last, tokens, normed, bias, total, up, down)
 
 
 def finish_own_kernel(first, last, normed, bias, before, up, down, hidden, fc2_bias, total):
     def body(rows, _):
         total[rows] = before[rows] + hidden[rows].astype(jnp.float32) + fc2_bias[...].reshape(1, -1)
 
-    over_blocks(before.shape[0], body)
-    add_tiles(first, last, normed, bias, total, up, down)
+    over_blocks(total.shape[0], body)
+    add_tiles(first, last, 0, normed, bias, total, up, down)
 
 
 def unit_kernel(here_part, there_part, gain, shift, mask, head, head_bias, unit, pooled):
@@ -352,10 +364,14 @@
         scratch_shapes=[pltpu.SemaphoreType.DMA((2, 6))],
         name="parts",
     )(in_hbm(fc1_weight.T), in_hbm(fc2_weight))
+
     right_p = come_from(own_p, dx=1)
+    flip_q = come_from(own_q, dy=-1)
     left_p = come_from(own_p, dx=-1)
     flip_p = come_from(own_p, dy=1)
-    flip_q = come_from(own_q, dy=-1)
+    over_p = come_from(right_p, dx=1)
+    flip_right_p = come_from(right_p, dy=1)
+    flip_left_q = come_from(flip_q, dx=-1)
 
     places = (
         ((0, 0, 0), (0, 0, 1))
@@ -384,79 +400,65 @@
         out_specs=VMEM,
         name="norm",
     )(hidden, ln_gain, ln_bias)
-    normed = (normed, come_from(normed, dc=1))
-
-    def scratch(first, last):
-        return [pltpu.VMEM((last - first, width), jnp.bfloat16)] * 2
-
-    def add_units(first, last, totals, parts):
-        parts = parts[first // PART : -(-last // PART)]
-        before = (text_ids,) if totals is None else totals
-        keep = (pltpu.VMEM(text_ids.shape, jnp.float32),) if totals is None else ()
-        return kernel_of(
-            functools.partial(add_kernel, first, last, totals is None, len(parts))
-        )(
-            out_shape=(wide, wide) + keep,
-            in_specs=[VMEM] * (3 + len(before) + len(parts)),
-            out_specs=(VMEM,) * (2 + len(keep)),
-            scratch_shapes=scratch(first, last),
-            input_output_aliases={} if keep else {3: 0, 4: 1},
-            name=f"units_{first}_{last}",
-        )(*normed, bias, *before, *parts)
-
-    parts = (own_p, own_q)
-    *totals, keep = add_units(0, 256, None, parts)
-
-    image_emb = after(image_emb, normed[0])
-    images = image_emb.astype(jnp.float32)
+    other = come_from(normed, dc=1)
+    images = after(image_emb, normed).astype(jnp.float32)
     image_unit = (
         images * lax.rsqrt(jnp.sum(images * images, axis=-1, keepdims=True) + 1e-06)
     ).astype(jnp.bfloat16)
     pictures = [image_unit] + [come_from(image_unit, dz=d) for d in (1, 2, 3)]
 
-    wave = after((right_p, left_p, flip_p, flip_q), totals, pictures)
-    right_p, left_p, flip_p, flip_q = wave
-    parts = parts + wave
+    def scratch(first, last):
+        return [pltpu.VMEM((last - first, width), jnp.bfloat16)] * 2
+
+    both = pltpu.VMEM((2 * tokens, width), jnp.float32)
+    normed, total, keep = kernel_of(functools.partial(first_kernel, TILE))(
+        out_shape=(
+            pltpu.VMEM((2 * tokens, width), jnp.bfloat16),
+            both,
+            pltpu.VMEM(text_ids.shape, jnp.float32),
+        ),
+        in_specs=[VMEM] * 6,
+        out_specs=(VMEM,) * 3,
+        scratch_shapes=scratch(0, TILE),
+        name="units_first",
+    )(normed, other, bias, text_ids, own_p, own_q)
+
+    def add_units(first, last, total, parts, name):
+        parts = parts[first // PART : -(-last // PART)]
+        return kernel_of(functools.partial(add_kernel, first, last, len(parts)))(
+            out_shape=both,
+            in_specs=[VMEM] * (3 + len(parts)),
+            out_specs=VMEM,
+            scratch_shapes=scratch(first, last),
+            input_output_aliases={2: 0},
+            name=name,
+        )(normed, bias, total, *parts)
+
+    right_p, left_p, flip_p = after((right_p, left_p, flip_p), total, pictures)
     right_q = come_from(right_p, dz=1)
     left_q = come_from(left_p, dz=-1)
-    flip_right_p = come_from(right_p, dy=1)
     flip_left_p = come_from(left_p, dy=-1)
-    over_p = come_from(right_p, dx=1)
-    flip_left_q = come_from(flip_q, dx=-1)
-    totals = add_units(256, 768, totals, parts)
-
-    teacher_logits = after(teacher_logits, wave)
-    tiles = jnp.transpose(teacher_logits, (1, 2, 0))
-
+    parts = (own_p, own_q, right_p, left_p, flip_p, flip_q)
+    total = add_units(TILE, 768, total, parts, "units_second")
+
+    over_p, flip_right_p, flip_left_q = after((over_p, flip_right_p, flip_left_q), total)
+    flip_over_q = come_from(flip_left_q, dx=-1)
+    flip_right_q = come_from(flip_right_p, dz=1)
+    over_q = come_from(over_p, dz=-1)
+    flip_over_p = come_from(over_p, dy=1)
+
+    tiles = jnp.transpose(after(teacher_logits, total), (1, 2, 0))
     kinds = [pltpu.VMEM((n, *tiles.shape[1:]), tiles.dtype) for n in (4, 4, 8)]
     tiles_own, tiles_near, tiles_far = kernel_of(tile_kernel, 4)(
         out_shape=tuple(kinds), in_specs=[VMEM], out_specs=(VMEM,) * 3, name="tiles"
     )(tiles)
     tiles_far = come_from(tiles_far, dy=2)
 
-    wave = after(
-        (right_q, left_q, flip_right_p, flip_left_p, over_p, flip_left_q),
-        totals,
-        tiles_far,
-    )
-    right_q, left_q, flip_right_p, flip_left_p, over_p, flip_left_q = wave
-    parts = parts + wave
-    flip_right_q = come_from(flip_right_p, dz=1)
-    over_q = come_from(over_p, dz=-1)
-    flip_over_p = come_from(over_p, dy=1)
-    flip_over_q = come_from(flip_left_q, dx=-1)
-    tiles_swap = kernel_of(pack_kernel, 4)(
-        out_shape=pltpu.VMEM(tiles_far.shape, tiles_far.dtype),
-        in_specs=[VMEM] * 2,
-        out_specs=VMEM,
-        name="pack",
-    )(tiles_near, after(tiles_far, wave))
-    tile_sets = (tiles_own, tiles_far, come_from(tiles_swap, dc=1))
-    totals = add_units(768, 1536, totals, parts)
+    parts = parts + (right_q, left_q, flip_right_p, flip_left_p, over_p, flip_left_q)
+    total = add_units(768, 1536, total, parts, "units_third")
 
     first, last = 1536, units
-    parts = parts + after((flip_right_q, over_q, flip_over_p, flip_over_q), totals, tile_sets)
-    parts = parts[first // PART :]
+    parts = (parts + (flip_right_q, over_q, flip_over_p, flip_over_q))[first // PART :]
 
     rows = pltpu.VMEM((last - first, width), jnp.bfloat16)
     partial, up, down = kernel_of(
@@ -465,16 +467,15 @@
         out_shape=(wide, rows, rows),
         in_specs=[VMEM] * (3 + len(parts)),
         out_specs=(VMEM,) * 3,
-        input_output_aliases={2: 0},
         name="finish_other",
-    )(normed[1], bias, totals[1], *parts)
+    )(normed, bias, total, *parts)
     there_part = come_from(partial, dc=1)
     here_part = kernel_of(functools.partial(finish_own_kernel, first, last))(
         out_shape=wide,
         in_specs=[VMEM] * 7,
         out_specs=VMEM,
         name="finish_own",
-    )(normed[0], bias, totals[0], up, down, hidden, fc2_bias)
+    )(normed, bias, total, up, down, hidden, fc2_bias)
     text_unit = kernel_of(unit_kernel, 6)(
         out_shape=pltpu.VMEM((texts_here, width), jnp.bfloat16),
         in_specs=[VMEM] * 7,
@@ -488,6 +489,14 @@
     line = jnp.concatenate(near_x, axis=0)
     across = [across] + [come_from(across, dx=d) for d in NEAR[1:]]
     lines = [line, come_from(line, dy=1), jnp.concatenate(across, axis=0), come_from(line, dy=-1)]
+    tiles_near, tiles_far = after((tiles_near, tiles_far), text_unit)
+    tiles_swap = kernel_of(pack_kernel, 4)(
+        out_shape=pltpu.VMEM(tiles_far.shape, tiles_far.dtype),
+        in_specs=[VMEM] * 2,
+        out_specs=VMEM,
+        name="pack",
+    )(tiles_near, tiles_far)
+    tile_sets = (tiles_own, tiles_far, come_from(tiles_swap, dc=1))
     lines = lines + [come_from(part, dc=1) for part in lines]
     grads = kernel_of(score_kernel, 6)(
         out_shape=tuple(

time: 148 us -> 138 us (0.932)
  starting transfers between devices: 62.6 us -> 53.1 us
  waiting for transfers between devices: 32.8 us -> 35.9 us
    ppermute x37, starting transfers between devices: 62.6 us -> 53.1 us  [come_from(): return lax.ppermute(array, AXES, pairs)]
    ppermute x37, waiting for transfers between devices: 32.8 us -> 35.9 us  [come_from(): return lax.ppermute(array, AXES, pairs)]
    unnamed x36 -> x32, local copies, waits for them, and re-layouts: 3.44 us -> 2.5 us
  transfers between devices with their start and end apart: 37 -> 37, of which waited for: 10 -> 14; matrix products, arithmetic and copies ran while one was open for 2% -> 0% of each run, Pallas kernels for 20% -> 22%
where the time goes in v1:
time: 138 us; the launch traced here: 137 us
  starting transfers between devices  53.1 us (38%)
  Pallas kernels  42.8 us (31%)
  waiting for transfers between devices  35.9 us (26%)
  local copies, waits for them, and re-layouts  2.51 us (2%)
  between operations  1.63 us (1%)
    ppermute x37, starting transfers between devices, come_from(): return lax.ppermute(array, AXES, pairs)  53.1 us
    ppermute x37, waiting for transfers between devices, come_from(): return lax.ppermute(array, AXES, pairs)  35.9 us
    pallas_call x2, Pallas kernels, add_units(): kernel_of(functools.partial(add_kernel, first, last, len(parts)))  19 us
    pallas_call x1, Pallas kernels, on_device(): kernel_of(functools.partial(first_kernel, TILE))  5.13 us
    pallas_call x1, Pallas kernels, on_device(): kernel_of(functools.partial(finish_other_kernel, first, last, len(parts)))  5.09 us
    pallas_call x1, Pallas kernels, on_device(): kernel_of(functools.partial(finish_own_kernel, first, last))  5.04 us
  transfers between devices with their start and end apart: 37, of which 14 were waited for; matrix products, arithmetic and copies ran while one was open for 0% of the time, Pallas kernels for 22%

profile of v1, /device:TPU:1, one launch (start us, length us, event | category | flops | bytes accessed | tf_op | source)
XLA Modules:
  0.0 136.8 jit_solution(16686297750195433941)
XLA Ops:
  3.5 3.3 %collective-permute-start = (bf16[512,1152]{1,0:T(8,128)(2,1)S(1)}, bf16[512,1152]{1,0:T(8,128)(2,1)S(1)}, u32[]{:S(2)}, u32[]{:S(2)}) collective-permute-start(bf16[512,1152]{1,0:T(8,128)(2,1)S(1)} %norm.1.own), channel_id=1, source_target_pairs={{8,0},{9,1},{10,2},{11,3},{12,4},{13,5},{14,6},{15,7},{0,8},{1,9},... | collective-permute-start | bytes 3538952 | tf_op jit(solution)/shard_map/ppermute | solution.py:32
  7.0 4.0 %collective-permute-start.4 = (bf16[32,1152]{1,0:T(8,128)(2,1)S(1)}, bf16[32,1152]{1,0:T(8,128)(2,1)S(1)}, u32[]{:S(2)}, u32[]{:S(2)}) collective-permute-start(bf16[32,1152]{1,0:T(8,128)(2,1)S(1)} %fusion.1.refs_8_), channel_id=1, source_target_pairs={{32,0},{33,1},{34,2},{35,3},{36,4},{37,5},{38,6},{39,7},{40,8},{41... | collective-permute-start | bytes 221192 | tf_op jit(solution)/shard_map/ppermute | solution.py:32
  12.1 2.5 %collective-permute-start.1 = (bf16[272,1152]{1,0:T(8,128)(2,1)}, bf16[272,1152]{1,0:T(8,128)(2,1)}, u32[]{:S(2)}, u32[]{:S(2)}) collective-permute-start(bf16[272,1152]{1,0:T(8,128)(2,1)} %get-tuple-element.31.part_p), channel_id=1, source_target_pairs={{1,0},{2,1},{3,2},{0,3},{5,4},{6,5},{7,6},{4,7},{9,8},{10,9},{11,1... | collective-permute-start | bytes 1880072 | tf_op jit(solution)/shard_map/ppermute | solution.py:32
  19.2 2.4 %collective-permute-start.6 = (bf16[32,1152]{1,0:T(8,128)(2,1)S(1)}, bf16[32,1152]{1,0:T(8,128)(2,1)S(1)}, u32[]{:S(2)}, u32[]{:S(2)}) collective-permute-start(bf16[32,1152]{1,0:T(8,128)(2,1)S(1)} %fusion.1.refs_8_), channel_id=1, source_target_pairs={{96,0},{97,1},{98,2},{99,3},{100,4},{101,5},{102,6},{103,7},{104,8... | collective-permute-start | bytes 221192 | tf_op jit(solution)/shard_map/ppermute | solution.py:32
  23.1 5.1 %units_first.1 = (bf16[1024,1152]{1,0:T(8,128)(2,1)S(1)}, f32[1024,1152]{1,0:T(8,128)S(1)}, f32[32,16]{1,0:T(8,128)S(1)}) custom-call(bf16[512,1152]{1,0:T(8,128)(2,1)S(1)} %norm.1.own, bf16[512,1152]{1,0:T(8,128)(2,1)S(1)} %copy-done.3, f32[9,256]{1,0:T(8,128)S(1)} %bias.1, s32[32,16]{1,0:T(8,128)S(1)} %copy.19.ids, ...), custom_call_target="tpu_custom_call" | custom-call | tf_op jit(solution)/shard_map/units_first/pallas_call | solution.py:414
  28.3 2.9 %collective-permute-start.10 = (bf16[272,1152]{1,0:T(8,128)(2,1)}, bf16[272,1152]{1,0:T(8,128)(2,1)S(1)}, u32[]{:S(2)}, u32[]{:S(2)}) collective-permute-start(bf16[272,1152]{1,0:T(8,128)(2,1)} %collective-permute-done.1.refs_1_), channel_id=1, source_target_pairs={{1,0},{2,1},{3,2},{0,3},{5,4},{6,5},{7,6},{4,7},{9,8},{10,9},{11,1... | collective-permute-start | bytes 1880072 | tf_op jit(solution)/shard_map/ppermute | solution.py:32
  31.2 2.7 %collective-permute-start.11 = (bf16[272,1152]{1,0:T(8,128)(2,1)}, bf16[272,1152]{1,0:T(8,128)(2,1)S(1)}, u32[]{:S(2)}, u32[]{:S(2)}) collective-permute-start(bf16[272,1152]{1,0:T(8,128)(2,1)} %collective-permute-done.1.refs_1_), channel_id=1, source_target_pairs={{4,0},{5,1},{6,2},{7,3},{16,4},{17,5},{18,6},{19,7},{12,8},{13,9},... | collective-permute-start | bytes 1880072 | tf_op jit(solution)/shard_map/ppermute | solution.py:32
  35.1 8.1 %units_second.1._ = f32[1024,1152]{1,0:T(8,128)S(1)} custom-call(bf16[1024,1152]{1,0:T(8,128)(2,1)S(1)} %get-tuple-element.34.normed, f32[9,256]{1,0:T(8,128)S(1)} %bias.1, f32[1024,1152]{1,0:T(8,128)S(1)} %get-tuple-element.35._, bf16[272,1152]{1,0:T(8,128)(2,1)S(1)} %get-tuple-element.33.part_q.refs_0_, ...), custom_call_target="tpu_custom_call", output_to_operand_aliasing={{}: (2, {})} | custom-call | tf_op jit(solution)/shard_map/units_second/pallas_call | solution.py:428
  46.1 3.0 %collective-permute-done.12.refs_6_.refs_0_ = bf16[272,1152]{1,0:T(8,128)(2,1)S(1)} collective-permute-done((bf16[272,1152]{1,0:T(8,128)(2,1)}, bf16[272,1152]{1,0:T(8,128)(2,1)S(1)}, u32[]{:S(2)}, u32[]{:S(2)}) %collective-permute-start.12) | collective-permute-done | bytes 626720 | tf_op jit(solution)/shard_map/ppermute | solution.py:32
  52.7 5.6 %collective-permute-done.8.refs_1_ = bf16[272,1152]{1,0:T(8,128)(2,1)S(1)} collective-permute-done((bf16[272,1152]{1,0:T(8,128)(2,1)}, bf16[272,1152]{1,0:T(8,128)(2,1)S(1)}, u32[]{:S(2)}, u32[]{:S(2)}) %collective-permute-start.8) | collective-permute-done | bytes 626720 | tf_op jit(solution)/shard_map/ppermute | solution.py:32
  58.3 10.8 %units_third.1.before = f32[1024,1152]{1,0:T(8,128)S(1)} custom-call(bf16[1024,1152]{1,0:T(8,128)(2,1)S(1)} %get-tuple-element.34.normed, f32[9,256]{1,0:T(8,128)S(1)} %bias.1, f32[1024,1152]{1,0:T(8,128)S(1)} %units_second.1._, bf16[272,1152]{1,0:T(8,128)(2,1)} %collective-permute-done.7.refs_4_.refs_0_, ...), custom_call_target="tpu_custom_call", output_to_operand_aliasing={{}: (2, {})} | custom-call | tf_op jit(solution)/shard_map/units_third/pallas_call | solution.py:428
  69.1 2.6 %collective-permute-done.14.refs_1_ = bf16[272,1152]{1,0:T(8,128)(2,1)S(1)} collective-permute-done((bf16[272,1152]{1,0:T(8,128)(2,1)S(1)}, bf16[272,1152]{1,0:T(8,128)(2,1)S(1)}, u32[]{:S(2)}, u32[]{:S(2)}) %collective-permute-start.14) | collective-permute-done | bytes 626720 | tf_op jit(solution)/shard_map/ppermute | solution.py:32
  71.7 5.1 %finish_other.1 = (f32[512,1152]{1,0:T(8,128)S(1)}, bf16[640,1152]{1,0:T(8,128)(2,1)S(1)}, bf16[640,1152]{1,0:T(8,128)(2,1)S(1)}) custom-call(bf16[1024,1152]{1,0:T(8,128)(2,1)S(1)} %get-tuple-element.34.normed, f32[9,256]{1,0:T(8,128)S(1)} %bias.1, f32[1024,1152]{1,0:T(8,128)S(1)} %units_third.1.before, ...), custom_call_target="tpu_custom_call" | custom-call | tf_op jit(solution)/shard_map/finish_other/pallas_call | solution.py:464
  76.8 2.9 %collective-permute-start.18 = (f32[512,1152]{1,0:T(8,128)S(1)}, f32[512,1152]{1,0:T(8,128)S(1)}, u32[]{:S(2)}, u32[]{:S(2)}) collective-permute-start(f32[512,1152]{1,0:T(8,128)S(1)} %get-tuple-element.45), channel_id=1, source_target_pairs={{8,0},{9,1},{10,2},{11,3},{12,4},{13,5},{14,6},{15,7},{0,8},{1,9},... | collective-permute-start | bytes 7077896 | tf_op jit(solution)/shard_map/ppermute | solution.py:32
  79.7 5.0 %finish_own.1.here_part = f32[512,1152]{1,0:T(8,128)S(1)} custom-call(bf16[1024,1152]{1,0:T(8,128)(2,1)S(1)} %get-tuple-element.34.normed, f32[9,256]{1,0:T(8,128)S(1)} %bias.1, f32[1024,1152]{1,0:T(8,128)S(1)} %units_third.1.before, bf16[640,1152]{1,0:T(8,128)(2,1)S(1)} %get-tuple-element.43.up, bf16[640,1152]{1,0:T(8,128)(2,1)S(1)} %get-tuple-element.44.down, ...), custom_call_target="tpu_custom_call" | custom-call | tf_op jit(solution)/shard_map/finish_own/pallas_call | solution.py:473
  87.0 3.4 %collective-permute-start.19 = (bf16[32,1152]{1,0:T(8,128)(2,1)S(1)}, bf16[32,1152]{1,0:T(8,128)(2,1)S(1)}, u32[]{:S(2)}, u32[]{:S(2)}) collective-permute-start(bf16[32,1152]{1,0:T(8,128)(2,1)S(1)} %unit.1), channel_id=1, source_target_pairs={{1,0},{2,1},{3,2},{0,3},{5,4},{6,5},{7,6},{4,7},{9,8},{10,9},{11,1... | collective-permute-start | bytes 221192 | tf_op jit(solution)/shard_map/ppermute | solution.py:32
  91.3 2.4 %collective-permute-start.23 = (bf16[32,1152]{1,0:T(8,128)(2,1)S(1)}, bf16[32,1152]{1,0:T(8,128)(2,1)S(1)}, u32[]{:S(2)}, u32[]{:S(2)}) collective-permute-start(bf16[32,1152]{1,0:T(8,128)(2,1)S(1)} %unit.1), channel_id=1, source_target_pairs={{16,0},{17,1},{18,2},{19,3},{20,4},{21,5},{22,6},{23,7},{24,8},{25... | collective-permute-start | bytes 221192 | tf_op jit(solution)/shard_map/ppermute | solution.py:32
  101.1 3.1 %collective-permute-done.24 = bf16[32,1152]{1,0:T(8,128)(2,1)S(1)} collective-permute-done((bf16[32,1152]{1,0:T(8,128)(2,1)S(1)}, bf16[32,1152]{1,0:T(8,128)(2,1)S(1)}, u32[]{:S(2)}, u32[]{:S(2)}) %collective-permute-start.24) | collective-permute-done | bytes 73760 | tf_op jit(solution)/shard_map/ppermute | solution.py:32
  105.7 3.2 %collective-permute-done.26 = bf16[32,1152]{1,0:T(8,128)(2,1)S(1)} collective-permute-done((bf16[32,1152]{1,0:T(8,128)(2,1)S(1)}, bf16[32,1152]{1,0:T(8,128)(2,1)S(1)}, u32[]{:S(2)}, u32[]{:S(2)}) %collective-permute-start.26) | collective-permute-done | bytes 73760 | tf_op jit(solution)/shard_map/ppermute | solution.py:32
  108.9 2.4 %collective-permute-start.30 = (bf16[128,1152]{1,0:T(8,128)(2,1)S(1)}, bf16[128,1152]{1,0:T(8,128)(2,1)S(1)}, u32[]{:S(2)}, u32[]{:S(2)}) collective-permute-start(bf16[128,1152]{1,0:T(8,128)(2,1)S(1)} %constant_dynamic-update-slice_fusion.refs_2_), channel_id=1, source_target_pairs={{8,0},{9,1},{10,2},{11,3},{12,4},{13,5},{14,6},{15,7},{0,8},{1,9},... | collective-permute-start | bytes 884744 | tf_op jit(solution)/shard_map/ppermute | solution.py:32
  113.9 4.6 %collective-permute-done.32.far.refs_13_ = bf16[8,32,256]{2,1,0:T(8,128)(2,1)S(1)} collective-permute-done((bf16[8,32,256]{2,1,0:T(8,128)(2,1)S(1)}, bf16[8,32,256]{2,1,0:T(8,128)(2,1)S(1)}, u32[]{:S(2)}, u32[]{:S(2)}) %collective-permute-start.32) | collective-permute-done | bytes 131104 | tf_op jit(solution)/shard_map/ppermute | solution.py:32
  120.9 2.6 %scores.1 = (f32[32,1152]{1,0:T(8,128)S(1)}, bf16[32,1152]{1,0:T(8,128)(2,1)S(1)}, bf16[32,1152]{1,0:T(8,128)(2,1)S(1)}, bf16[32,1152]{1,0:T(8,128)(2,1)S(1)}) custom-call(f32[1]{0:T(128)} %copy.25.logit_scale, f32[1]{0:T(128)S(6)} %copy.26.logit_bias, bf16[128,1152]{1,0:T(8,128)(2,1)S(1)} %pad_maximum_fusion.refs_0_, ...), custom_call_target="tpu_custom_call" | custom-call | tf_op jit(solution)/shard_map/scores/pallas_call | solution.py:501
  128.7 5.0 %collective-permute-done.35 = bf16[32,1152]{1,0:T(8,128)(2,1)S(1)} collective-permute-done((bf16[32,1152]{1,0:T(8,128)(2,1)S(1)}, bf16[32,1152]{1,0:T(8,128)(2,1)S(1)}, u32[]{:S(2)}, u32[]{:S(2)}) %collective-permute-start.35) | collective-permute-done | bytes 73760 | tf_op jit(solution)/shard_map/ppermute | solution.py:32
  133.6 2.5 %collective-permute-done.36 = bf16[32,1152]{1,0:T(8,128)(2,1)S(1)} collective-permute-done((bf16[32,1152]{1,0:T(8,128)(2,1)S(1)}, bf16[32,1152]{1,0:T(8,128)(2,1)S(1)}, u32[]{:S(2)}, u32[]{:S(2)}) %collective-permute-start.36) | collective-permute-done | bytes 73760 | tf_op jit(solution)/shard_map/ppermute | solution.py:32
  (100 shorter events, 39.9 us)
Async XLA Ops:
  3.5 14.6 %collective-permute-start = (bf16[512,1152]{1,0:T(8,128)(2,1)S(1)}, bf16[512,1152]{1,0:T(8,128)(2,1)S(1)}, u32[]{:S(2)}, u32[]{:S(2)}) collective-permute-start(bf16[512,1152]{1,0:T(8,128)(2,1)S(1)} %norm.1.own), channel_id=1, source_target_pairs={{8,0},{9,1},{10,2},{11,3},{12,4},{13,5},{14,6},{15,7},{0,8},{1,9},... | collective-permute-start | bytes 3538952 | tf_op jit(solution)/shard_map/ppermute | solution.py:32
  12.1 16.1 %collective-permute-start.1 = (bf16[272,1152]{1,0:T(8,128)(2,1)}, bf16[272,1152]{1,0:T(8,128)(2,1)}, u32[]{:S(2)}, u32[]{:S(2)}) collective-permute-start(bf16[272,1152]{1,0:T(8,128)(2,1)} %get-tuple-element.31.part_p), channel_id=1, source_target_pairs={{1,0},{2,1},{3,2},{0,3},{5,4},{6,5},{7,6},{4,7},{9,8},{10,9},{11,1... | collective-permute-start | bytes 1880072 | tf_op jit(solution)/shard_map/ppermute | solution.py:32
  14.6 19.4 %collective-permute-start.7 = (bf16[272,1152]{1,0:T(8,128)(2,1)S(1)}, bf16[272,1152]{1,0:T(8,128)(2,1)}, u32[]{:S(2)}, u32[]{:S(2)}) collective-permute-start(bf16[272,1152]{1,0:T(8,128)(2,1)S(1)} %get-tuple-element.33.part_q.refs_0_), channel_id=1, source_target_pairs={{20,0},{21,1},{22,2},{23,3},{0,4},{1,5},{2,6},{3,7},{28,8},{29,9},... | collective-permute-start | bytes 1880072 | tf_op jit(solution)/shard_map/ppermute | solution.py:32
  15.9 18.1 %collective-permute-start.2 = (bf16[272,1152]{1,0:T(8,128)(2,1)}, bf16[272,1152]{1,0:T(8,128)(2,1)}, u32[]{:S(2)}, u32[]{:S(2)}) collective-permute-start(bf16[272,1152]{1,0:T(8,128)(2,1)} %get-tuple-element.31.part_p), channel_id=1, source_target_pairs={{3,0},{0,1},{1,2},{2,3},{7,4},{4,5},{5,6},{6,7},{11,8},{8,9},{9,10... | collective-permute-start | bytes 1880072 | tf_op jit(solution)/shard_map/ppermute | solution.py:32
  15.9 18.1 %collective-permute-start.3 = (bf16[272,1152]{1,0:T(8,128)(2,1)}, bf16[272,1152]{1,0:T(8,128)(2,1)}, u32[]{:S(2)}, u32[]{:S(2)}) collective-permute-start(bf16[272,1152]{1,0:T(8,128)(2,1)} %get-tuple-element.31.part_p), channel_id=1, source_target_pairs={{4,0},{5,1},{6,2},{7,3},{16,4},{17,5},{18,6},{19,7},{12,8},{13,9},... | collective-permute-start | bytes 1880072 | tf_op jit(solution)/shard_map/ppermute | solution.py:32
  19.2 12.0 %collective-permute-start.6 = (bf16[32,1152]{1,0:T(8,128)(2,1)S(1)}, bf16[32,1152]{1,0:T(8,128)(2,1)S(1)}, u32[]{:S(2)}, u32[]{:S(2)}) collective-permute-start(bf16[32,1152]{1,0:T(8,128)(2,1)S(1)} %fusion.1.refs_8_), channel_id=1, source_target_pairs={{96,0},{97,1},{98,2},{99,3},{100,4},{101,5},{102,6},{103,7},{104,8... | collective-permute-start | bytes 221192 | tf_op jit(solution)/shard_map/ppermute | solution.py:32
  28.3 15.3 %collective-permute-start.10 = (bf16[272,1152]{1,0:T(8,128)(2,1)}, bf16[272,1152]{1,0:T(8,128)(2,1)S(1)}, u32[]{:S(2)}, u32[]{:S(2)}) collective-permute-start(bf16[272,1152]{1,0:T(8,128)(2,1)} %collective-permute-done.1.refs_1_), channel_id=1, source_target_pairs={{1,0},{2,1},{3,2},{0,3},{5,4},{6,5},{7,6},{4,7},{9,8},{10,9},{11,1... | collective-permute-start | bytes 1880072 | tf_op jit(solution)/shard_map/ppermute | solution.py:32
  31.2 14.8 %collective-permute-start.11 = (bf16[272,1152]{1,0:T(8,128)(2,1)}, bf16[272,1152]{1,0:T(8,128)(2,1)S(1)}, u32[]{:S(2)}, u32[]{:S(2)}) collective-permute-start(bf16[272,1152]{1,0:T(8,128)(2,1)} %collective-permute-done.1.refs_1_), channel_id=1, source_target_pairs={{4,0},{5,1},{6,2},{7,3},{16,4},{17,5},{18,6},{19,7},{12,8},{13,9},... | collective-permute-start | bytes 1880072 | tf_op jit(solution)/shard_map/ppermute | solution.py:32
  34.0 15.1 %collective-permute-start.12 = (bf16[272,1152]{1,0:T(8,128)(2,1)}, bf16[272,1152]{1,0:T(8,128)(2,1)S(1)}, u32[]{:S(2)}, u32[]{:S(2)}) collective-permute-start(bf16[272,1152]{1,0:T(8,128)(2,1)} %collective-permute-done.7.refs_4_.refs_0_), channel_id=1, source_target_pairs={{3,0},{0,1},{1,2},{2,3},{7,4},{4,5},{5,6},{6,7},{11,8},{8,9},{9,10... | collective-permute-start | bytes 1880072 | tf_op jit(solution)/shard_map/ppermute | solution.py:32
  34.0 16.3 %collective-permute-start.13 = (bf16[272,1152]{1,0:T(8,128)(2,1)}, bf16[272,1152]{1,0:T(8,128)(2,1)S(1)}, u32[]{:S(2)}, u32[]{:S(2)}) collective-permute-start(bf16[272,1152]{1,0:T(8,128)(2,1)} %collective-permute-done.2.refs_2_), channel_id=1, source_target_pairs={{20,0},{21,1},{22,2},{23,3},{0,4},{1,5},{2,6},{3,7},{28,8},{29,9},... | collective-permute-start | bytes 1880072 | tf_op jit(solution)/shard_map/ppermute | solution.py:32
  34.1 18.1 %collective-permute-start.9 = (bf16[272,1152]{1,0:T(8,128)(2,1)}, bf16[272,1152]{1,0:T(8,128)(2,1)S(1)}, u32[]{:S(2)}, u32[]{:S(2)}) collective-permute-start(bf16[272,1152]{1,0:T(8,128)(2,1)} %collective-permute-done.2.refs_2_), channel_id=1, source_target_pairs={{224,0},{225,1},{226,2},{227,3},{228,4},{229,5},{230,6},{231,7},{2... | collective-permute-start | bytes 1880072 | tf_op jit(solution)/shard_map/ppermute | solution.py:32
  43.6 14.7 %collective-permute-start.8 = (bf16[272,1152]{1,0:T(8,128)(2,1)}, bf16[272,1152]{1,0:T(8,128)(2,1)S(1)}, u32[]{:S(2)}, u32[]{:S(2)}) collective-permute-start(bf16[272,1152]{1,0:T(8,128)(2,1)} %collective-permute-done.1.refs_1_), channel_id=1, source_target_pairs={{32,0},{33,1},{34,2},{35,3},{36,4},{37,5},{38,6},{39,7},{40,8},{41... | collective-permute-start | bytes 1880072 | tf_op jit(solution)/shard_map/ppermute | solution.py:32
  49.1 22.6 %collective-permute-start.15 = (bf16[272,1152]{1,0:T(8,128)(2,1)S(1)}, bf16[272,1152]{1,0:T(8,128)(2,1)S(1)}, u32[]{:S(2)}, u32[]{:S(2)}) collective-permute-start(bf16[272,1152]{1,0:T(8,128)(2,1)S(1)} %collective-permute-done.10.refs_5_), channel_id=1, source_target_pairs={{224,0},{225,1},{226,2},{227,3},{228,4},{229,5},{230,6},{231,7},{2... | collective-permute-start | bytes 1880072 | tf_op jit(solution)/shard_map/ppermute | solution.py:32
  49.8 21.9 %collective-permute-start.16 = (bf16[272,1152]{1,0:T(8,128)(2,1)S(1)}, bf16[272,1152]{1,0:T(8,128)(2,1)S(1)}, u32[]{:S(2)}, u32[]{:S(2)}) collective-permute-start(bf16[272,1152]{1,0:T(8,128)(2,1)S(1)} %collective-permute-done.10.refs_5_), channel_id=1, source_target_pairs={{4,0},{5,1},{6,2},{7,3},{16,4},{17,5},{18,6},{19,7},{12,8},{13,9},... | collective-permute-start | bytes 1880072 | tf_op jit(solution)/shard_map/ppermute | solution.py:32
  50.3 21.4 %collective-permute-start.14 = (bf16[272,1152]{1,0:T(8,128)(2,1)S(1)}, bf16[272,1152]{1,0:T(8,128)(2,1)S(1)}, u32[]{:S(2)}, u32[]{:S(2)}) collective-permute-start(bf16[272,1152]{1,0:T(8,128)(2,1)S(1)} %collective-permute-done.11.refs_3_), channel_id=1, source_target_pairs={{32,0},{33,1},{34,2},{35,3},{36,4},{37,5},{38,6},{39,7},{40,8},{41... | collective-permute-start | bytes 1880072 | tf_op jit(solution)/shard_map/ppermute | solution.py:32
  52.2 19.5 %collective-permute-start.17 = (bf16[272,1152]{1,0:T(8,128)(2,1)S(1)}, bf16[272,1152]{1,0:T(8,128)(2,1)S(1)}, u32[]{:S(2)}, u32[]{:S(2)}) collective-permute-start(bf16[272,1152]{1,0:T(8,128)(2,1)S(1)} %collective-permute-done.12.refs_6_.refs_0_), channel_id=1, source_target_pairs={{3,0},{0,1},{1,2},{2,3},{7,4},{4,5},{5,6},{6,7},{11,8},{8,9},{9,10... | collective-permute-start | bytes 1880072 | tf_op jit(solution)/shard_map/ppermute | solution.py:32
  91.3 9.2 %collective-permute-start.23 = (bf16[32,1152]{1,0:T(8,128)(2,1)S(1)}, bf16[32,1152]{1,0:T(8,128)(2,1)S(1)}, u32[]{:S(2)}, u32[]{:S(2)}) collective-permute-start(bf16[32,1152]{1,0:T(8,128)(2,1)S(1)} %unit.1), channel_id=1, source_target_pairs={{16,0},{17,1},{18,2},{19,3},{20,4},{21,5},{22,6},{23,7},{24,8},{25... | collective-permute-start | bytes 221192 | tf_op jit(solution)/shard_map/ppermute | solution.py:32
  97.1 14.2 %collective-permute-start.22 = (bf16[128,1152]{1,0:T(8,128)(2,1)S(1)}, bf16[128,1152]{1,0:T(8,128)(2,1)S(1)}, u32[]{:S(2)}, u32[]{:S(2)}) collective-permute-start(bf16[128,1152]{1,0:T(8,128)(2,1)S(1)} %pad_maximum_fusion.refs_0_), channel_id=1, source_target_pairs={{4,0},{5,1},{6,2},{7,3},{16,4},{17,5},{18,6},{19,7},{12,8},{13,9},... | collective-permute-start | bytes 884744 | tf_op jit(solution)/shard_map/ppermute | solution.py:32
  99.4 12.1 %collective-permute-start.27 = (bf16[128,1152]{1,0:T(8,128)(2,1)S(1)}, bf16[128,1152]{1,0:T(8,128)(2,1)S(1)}, u32[]{:S(2)}, u32[]{:S(2)}) collective-permute-start(bf16[128,1152]{1,0:T(8,128)(2,1)S(1)} %pad_maximum_fusion.refs_0_), channel_id=1, source_target_pairs={{20,0},{21,1},{22,2},{23,3},{0,4},{1,5},{2,6},{3,7},{28,8},{29,9},... | collective-permute-start | bytes 884744 | tf_op jit(solution)/shard_map/ppermute | solution.py:32
  99.4 21.5 %collective-permute-start.28 = (bf16[128,1152]{1,0:T(8,128)(2,1)S(1)}, bf16[128,1152]{1,0:T(8,128)(2,1)S(1)}, u32[]{:S(2)}, u32[]{:S(2)}) collective-permute-start(bf16[128,1152]{1,0:T(8,128)(2,1)S(1)} %pad_maximum_fusion.refs_0_), channel_id=1, source_target_pairs={{8,0},{9,1},{10,2},{11,3},{12,4},{13,5},{14,6},{15,7},{0,8},{1,9},... | collective-permute-start | bytes 884744 | tf_op jit(solution)/shard_map/ppermute | solution.py:32
  108.9 12.0 %collective-permute-start.30 = (bf16[128,1152]{1,0:T(8,128)(2,1)S(1)}, bf16[128,1152]{1,0:T(8,128)(2,1)S(1)}, u32[]{:S(2)}, u32[]{:S(2)}) collective-permute-start(bf16[128,1152]{1,0:T(8,128)(2,1)S(1)} %constant_dynamic-update-slice_fusion.refs_2_), channel_id=1, source_target_pairs={{8,0},{9,1},{10,2},{11,3},{12,4},{13,5},{14,6},{15,7},{0,8},{1,9},... | collective-permute-start | bytes 884744 | tf_op jit(solution)/shard_map/ppermute | solution.py:32
  111.3 9.6 %collective-permute-start.29 = (bf16[128,1152]{1,0:T(8,128)(2,1)S(1)}, bf16[128,1152]{1,0:T(8,128)(2,1)S(1)}, u32[]{:S(2)}, u32[]{:S(2)}) collective-permute-start(bf16[128,1152]{1,0:T(8,128)(2,1)S(1)} %collective-permute-done.22.refs_1_), channel_id=1, source_target_pairs={{8,0},{9,1},{10,2},{11,3},{12,4},{13,5},{14,6},{15,7},{0,8},{1,9},... | collective-permute-start | bytes 884744 | tf_op jit(solution)/shard_map/ppermute | solution.py:32
  111.4 9.5 %collective-permute-start.31 = (bf16[128,1152]{1,0:T(8,128)(2,1)S(1)}, bf16[128,1152]{1,0:T(8,128)(2,1)S(1)}, u32[]{:S(2)}, u32[]{:S(2)}) collective-permute-start(bf16[128,1152]{1,0:T(8,128)(2,1)S(1)} %collective-permute-done.27.refs_3_), channel_id=1, source_target_pairs={{8,0},{9,1},{10,2},{11,3},{12,4},{13,5},{14,6},{15,7},{0,8},{1,9},... | collective-permute-start | bytes 884744 | tf_op jit(solution)/shard_map/ppermute | solution.py:32
  126.8 9.3 %collective-permute-start.36 = (bf16[32,1152]{1,0:T(8,128)(2,1)S(1)}, bf16[32,1152]{1,0:T(8,128)(2,1)S(1)}, u32[]{:S(2)}, u32[]{:S(2)}) collective-permute-start(bf16[32,1152]{1,0:T(8,128)(2,1)S(1)} %get-tuple-element.56), channel_id=1, source_target_pairs={{160,0},{161,1},{162,2},{163,3},{164,4},{165,5},{166,6},{167,7},{1... | collective-permute-start | bytes 221192 | tf_op jit(solution)/shard_map/ppermute | solution.py:32
  (27 other events, 193.7 us)

commit v2 on v1

--- a/solution.py
+++ b/solution.py
@@ -44,8 +44,7 @@
 
 
 BLOCK = 128
-ROWS_STEP = 512
-SHORT_STEP = 256
+ROWS_STEP = 256
 
 
 def over_blocks(tokens, body):
@@ -149,10 +148,26 @@
                     copy.wait() if waiting else copy.start()
 
 
-def add_term(first, tile, size, rows, normed, bias, up, down):
-    units = pl.ds(tile * TILE, size)
-    act = hidden_units(normed[rows], up[units], bias[pl.ds(first // TILE + tile, 1)][:, :size])
-    return jnp.dot(act, down[units], preferred_element_type=jnp.float32)
+def add_tiles(first, last, base, normed, bias, before, total, up, down):
+    step_rows = min(total.shape[0], ROWS_STEP)
+
+    def step(i, carry):
+        start = pl.multiple_of(i * step_rows, step_rows)
+        rows = pl.ds(base + start, step_rows)
+        here = pl.ds(start, step_rows)
+        for unit in range(0, last - first, TILE):
+            size = min(TILE, last - first - unit)
+            units = pl.ds(unit, size)
+            tile_bias = bias[pl.ds((first + unit) // TILE, 1)][:, :size]
+            act = hidden_units(normed[rows], up[units], tile_bias)
+            term = jnp.dot(act, down[units], preferred_element_type=jnp.float32)
+            if unit:
+                total[here] += term
+            else:
+                total[here] = term if before is None else before[rows] + term
+        return carry
+
+    lax.fori_loop(0, total.shape[0] // step_rows, step, 0)
 
 
 def first_kernel(last, own, other, bias, ids, part_p, part_q, normed, total, mask, up, down):
@@ -161,57 +176,19 @@
     normed[:count] = own[...]
     normed[count:] = other[...]
     assemble(0, last, (part_p, part_q), up, down)
-
-    def step(i, carry):
-        rows = pl.ds(pl.multiple_of(i * SHORT_STEP, SHORT_STEP), SHORT_STEP)
-        total[rows] = add_term(0, 0, TILE, rows, normed, bias, up, down)
-        return carry
-
-    lax.fori_loop(0, normed.shape[0] // SHORT_STEP, step, 0)
-
-
-def add_kernel(first, last, count, normed, bias, _, *refs):
+    add_tiles(0, last, 0, normed, bias, None, total, up, down)
+
+
+def add_kernel(first, last, count, normed, bias, before, *refs):
     parts, (total, up, down) = refs[:count], refs[count:]
     assemble(first, last, parts, up, down)
-    blocks = normed.shape[0] // ROWS_STEP
-
-    def step(i, carry):
-        rows = pl.ds(pl.multiple_of(i % blocks * ROWS_STEP, ROWS_STEP), ROWS_STEP)
-        total[rows] += add_term(first, i // blocks, TILE, rows, normed, bias, up, down)
-        return carry
-
-    lax.fori_loop(0, (last - first) // TILE * blocks, step, 0)
-
-
-def add_tiles(first, last, base, normed, bias, total, up, down):
-    steps = (last - first) // TILE
-    rest = last - first - steps * TILE
-    tokens = total.shape[0]
-
-    def step(tile, carry):
-        total[...] += add_term(first, tile, TILE, pl.ds(base, tokens), normed, bias, up, down)
-        return carry
-
-    lax.fori_loop(0, steps, step, 0)
-
-    def rest_step(i, carry):
-        start = pl.multiple_of(i * SHORT_STEP, SHORT_STEP)
-        rows = pl.ds(base + start, SHORT_STEP)
-        total[pl.ds(start, SHORT_STEP)] += add_term(
-            first, steps, rest, rows, normed, bias, up, down
-        )
-        return carry
-
-    if rest:
-        lax.fori_loop(0, tokens // SHORT_STEP, rest_step, 0)
+    add_tiles(first, last, 0, normed, bias, before, total, up, down)
 
 
 def finish_other_kernel(first, last, count, normed, bias, before, *refs):
     parts, (total, up, down) = refs[:count], refs[count:]
     assemble(first, last, parts, up, down)
-    tokens = total.shape[0]
-    total[...] = before[tokens:]
-    add_tiles(first, last, tokens, normed, bias, total, up, down)
+    add_tiles(first, last, total.shape[0], normed, bias, before, total, up, down)
 
 
 def finish_own_kernel(first, last, normed, bias, before, up, down, hidden, fc2_bias, total):
@@ -219,7 +196,7 @@
         total[rows] = before[rows] + hidden[rows].astype(jnp.float32) + fc2_bias[...].reshape(1, -1)
 
     over_blocks(total.shape[0], body)
-    add_tiles(first, last, 0, normed, bias, total, up, down)
+    add_tiles(first, last, 0, normed, bias, total, total, up, down)
 
 
 def unit_kernel(here_part, there_part, gain, shift, mask, head, head_bias, unit, pooled):
@@ -484,8 +461,8 @@
         name="unit",
     )(here_part, there_part, final_gain, final_bias, keep, head_weight, head_bias)
 
+    across = come_from(text_unit, dy=2)
     near_x = [text_unit] + [come_from(text_unit, dx=d) for d in NEAR[1:]]
-    across = come_from(text_unit, dy=2)
     line = jnp.concatenate(near_x, axis=0)
     across = [across] + [come_from(across, dx=d) for d in NEAR[1:]]
     lines = [line, come_from(line, dy=1), jnp.concatenate(across, axis=0), come_from(line, dy=-1)]

time: 138 us -> 136 us (0.986)
  Pallas kernels: 42.8 us -> 40 us
  waiting for transfers between devices: 35.9 us -> 37.5 us
    ppermute x37, waiting for transfers between devices: 35.9 us -> 37.5 us  [come_from(): return lax.ppermute(array, AXES, pairs)]
  transfers between devices with their start and end apart: 37 -> 37, of which waited for: 14 -> 15; matrix products, arithmetic and copies ran while one was open for 0% -> 0% of each run, Pallas kernels for 22% -> 21%
where the time goes in v2:
time: 136 us; the launch traced here: 134 us
  starting transfers between devices  51.9 us (38%)
  Pallas kernels  40 us (29%)
  waiting for transfers between devices  37.5 us (28%)
  local copies, waits for them, and re-layouts  2.51 us (2%)
  between operations  1.63 us (1%)
    ppermute x37, starting transfers between devices, come_from(): return lax.ppermute(array, AXES, pairs)  51.9 us
    ppermute x37, waiting for transfers between devices, come_from(): return lax.ppermute(array, AXES, pairs)  37.5 us
    pallas_call x2, Pallas kernels, add_units(): kernel_of(functools.partial(add_kernel, first, last, len(parts)))  17.8 us
    pallas_call x1, Pallas kernels, on_device(): kernel_of(functools.partial(first_kernel, TILE))  5.13 us
    pallas_call x1, Pallas kernels, on_device(): kernel_of(functools.partial(finish_own_kernel, first, last))  4.3 us
    pallas_call x1, Pallas kernels, on_device(): kernel_of(functools.partial(finish_other_kernel, first, last, len(parts)))  4.17 us
  transfers between devices with their start and end apart: 37, of which 15 were waited for; matrix products, arithmetic and copies ran while one was open for 0% of the time, Pallas kernels for 21%

profile of v2, /device:TPU:1, one launch (start us, length us, event | category | flops | bytes accessed | tf_op | source)
XLA Modules:
  0.0 134.5 jit_solution(10213026478512357357)
XLA Ops:
  0.0 2.3 %parts.1 = (bf16[272,1152]{1,0:T(8,128)(2,1)}, bf16[272,1152]{1,0:T(8,128)(2,1)S(1)}) custom-call(bf16[538,1152]{1,0:T(8,128)(2,1)} %bitcast.5, bf16[538,1152]{1,0:T(8,128)(2,1)} %downs.1), custom_call_target="tpu_custom_call" | custom-call | tf_op jit(solution)/shard_map/parts/pallas_call | solution.py:337
  3.5 3.3 %collective-permute-start = (bf16[512,1152]{1,0:T(8,128)(2,1)S(1)}, bf16[512,1152]{1,0:T(8,128)(2,1)S(1)}, u32[]{:S(2)}, u32[]{:S(2)}) collective-permute-start(bf16[512,1152]{1,0:T(8,128)(2,1)S(1)} %norm.1.own), channel_id=1, source_target_pairs={{8,0},{9,1},{10,2},{11,3},{12,4},{13,5},{14,6},{15,7},{0,8},{1,9},... | collective-permute-start | bytes 3538952 | tf_op jit(solution)/shard_map/ppermute | solution.py:32
  7.0 4.0 %collective-permute-start.4 = (bf16[32,1152]{1,0:T(8,128)(2,1)S(1)}, bf16[32,1152]{1,0:T(8,128)(2,1)S(1)}, u32[]{:S(2)}, u32[]{:S(2)}) collective-permute-start(bf16[32,1152]{1,0:T(8,128)(2,1)S(1)} %fusion.1.refs_8_), channel_id=1, source_target_pairs={{32,0},{33,1},{34,2},{35,3},{36,4},{37,5},{38,6},{39,7},{40,8},{41... | collective-permute-start | bytes 221192 | tf_op jit(solution)/shard_map/ppermute | solution.py:32
  12.1 2.5 %collective-permute-start.1 = (bf16[272,1152]{1,0:T(8,128)(2,1)}, bf16[272,1152]{1,0:T(8,128)(2,1)}, u32[]{:S(2)}, u32[]{:S(2)}) collective-permute-start(bf16[272,1152]{1,0:T(8,128)(2,1)} %get-tuple-element.31.part_p), channel_id=1, source_target_pairs={{1,0},{2,1},{3,2},{0,3},{5,4},{6,5},{7,6},{4,7},{9,8},{10,9},{11,1... | collective-permute-start | bytes 1880072 | tf_op jit(solution)/shard_map/ppermute | solution.py:32
  15.9 2.2 %collective-permute-start.3 = (bf16[272,1152]{1,0:T(8,128)(2,1)}, bf16[272,1152]{1,0:T(8,128)(2,1)}, u32[]{:S(2)}, u32[]{:S(2)}) collective-permute-start(bf16[272,1152]{1,0:T(8,128)(2,1)} %get-tuple-element.31.part_p), channel_id=1, source_target_pairs={{4,0},{5,1},{6,2},{7,3},{16,4},{17,5},{18,6},{19,7},{12,8},{13,9},... | collective-permute-start | bytes 1880072 | tf_op jit(solution)/shard_map/ppermute | solution.py:32
  19.2 2.4 %collective-permute-start.6 = (bf16[32,1152]{1,0:T(8,128)(2,1)S(1)}, bf16[32,1152]{1,0:T(8,128)(2,1)S(1)}, u32[]{:S(2)}, u32[]{:S(2)}) collective-permute-start(bf16[32,1152]{1,0:T(8,128)(2,1)S(1)} %fusion.1.refs_8_), channel_id=1, source_target_pairs={{96,0},{97,1},{98,2},{99,3},{100,4},{101,5},{102,6},{103,7},{104,8... | collective-permute-start | bytes 221192 | tf_op jit(solution)/shard_map/ppermute | solution.py:32
  23.1 5.1 %units_first.1 = (bf16[1024,1152]{1,0:T(8,128)(2,1)S(1)}, f32[1024,1152]{1,0:T(8,128)S(1)}, f32[32,16]{1,0:T(8,128)S(1)}) custom-call(bf16[512,1152]{1,0:T(8,128)(2,1)S(1)} %norm.1.own, bf16[512,1152]{1,0:T(8,128)(2,1)S(1)} %copy-done.3, f32[9,256]{1,0:T(8,128)S(1)} %bias.1, s32[32,16]{1,0:T(8,128)S(1)} %copy.19.ids, ...), custom_call_target="tpu_custom_call" | custom-call | tf_op jit(solution)/shard_map/units_first/pallas_call | solution.py:391
  28.3 2.9 %collective-permute-start.10 = (bf16[272,1152]{1,0:T(8,128)(2,1)}, bf16[272,1152]{1,0:T(8,128)(2,1)S(1)}, u32[]{:S(2)}, u32[]{:S(2)}) collective-permute-start(bf16[272,1152]{1,0:T(8,128)(2,1)} %collective-permute-done.1.refs_1_), channel_id=1, source_target_pairs={{1,0},{2,1},{3,2},{0,3},{5,4},{6,5},{7,6},{4,7},{9,8},{10,9},{11,1... | collective-permute-start | bytes 1880072 | tf_op jit(solution)/shard_map/ppermute | solution.py:32
  31.2 2.7 %collective-permute-start.11 = (bf16[272,1152]{1,0:T(8,128)(2,1)}, bf16[272,1152]{1,0:T(8,128)(2,1)S(1)}, u32[]{:S(2)}, u32[]{:S(2)}) collective-permute-start(bf16[272,1152]{1,0:T(8,128)(2,1)} %collective-permute-done.1.refs_1_), channel_id=1, source_target_pairs={{4,0},{5,1},{6,2},{7,3},{16,4},{17,5},{18,6},{19,7},{12,8},{13,9},... | collective-permute-start | bytes 1880072 | tf_op jit(solution)/shard_map/ppermute | solution.py:32
  35.1 7.9 %units_second.1.before = f32[1024,1152]{1,0:T(8,128)S(1)} custom-call(bf16[1024,1152]{1,0:T(8,128)(2,1)S(1)} %get-tuple-element.34.normed, f32[9,256]{1,0:T(8,128)S(1)} %bias.1, f32[1024,1152]{1,0:T(8,128)S(1)} %get-tuple-element.35.before, bf16[272,1152]{1,0:T(8,128)(2,1)S(1)} %get-tuple-element.33.part_q.refs_0_, ...), custom_call_target="tpu_custom_call", output_to_operand_aliasing={{}: (2, {})} | custom-call | tf_op jit(solution)/shard_map/units_second/pallas_call | solution.py:405
  46.1 3.0 %collective-permute-done.12.refs_6_.refs_0_ = bf16[272,1152]{1,0:T(8,128)(2,1)S(1)} collective-permute-done((bf16[272,1152]{1,0:T(8,128)(2,1)}, bf16[272,1152]{1,0:T(8,128)(2,1)S(1)}, u32[]{:S(2)}, u32[]{:S(2)}) %collective-permute-start.12) | collective-permute-done | bytes 626720 | tf_op jit(solution)/shard_map/ppermute | solution.py:32
  52.7 5.6 %collective-permute-done.8.refs_1_ = bf16[272,1152]{1,0:T(8,128)(2,1)S(1)} collective-permute-done((bf16[272,1152]{1,0:T(8,128)(2,1)}, bf16[272,1152]{1,0:T(8,128)(2,1)S(1)}, u32[]{:S(2)}, u32[]{:S(2)}) %collective-permute-start.8) | collective-permute-done | bytes 626720 | tf_op jit(solution)/shard_map/ppermute | solution.py:32
  58.3 9.9 %units_third.1.before = f32[1024,1152]{1,0:T(8,128)S(1)} custom-call(bf16[1024,1152]{1,0:T(8,128)(2,1)S(1)} %get-tuple-element.34.normed, f32[9,256]{1,0:T(8,128)S(1)} %bias.1, f32[1024,1152]{1,0:T(8,128)S(1)} %units_second.1.before, bf16[272,1152]{1,0:T(8,128)(2,1)} %collective-permute-done.7.refs_4_.refs_0_, ...), custom_call_target="tpu_custom_call", output_to_operand_aliasing={{}: (2, {})} | custom-call | tf_op jit(solution)/shard_map/units_third/pallas_call | solution.py:405
  68.2 3.5 %collective-permute-done.14.refs_1_ = bf16[272,1152]{1,0:T(8,128)(2,1)S(1)} collective-permute-done((bf16[272,1152]{1,0:T(8,128)(2,1)S(1)}, bf16[272,1152]{1,0:T(8,128)(2,1)S(1)}, u32[]{:S(2)}, u32[]{:S(2)}) %collective-permute-start.14) | collective-permute-done | bytes 626720 | tf_op jit(solution)/shard_map/ppermute | solution.py:32
  71.7 4.2 %finish_other.1 = (f32[512,1152]{1,0:T(8,128)S(1)}, bf16[640,1152]{1,0:T(8,128)(2,1)S(1)}, bf16[640,1152]{1,0:T(8,128)(2,1)S(1)}) custom-call(bf16[1024,1152]{1,0:T(8,128)(2,1)S(1)} %get-tuple-element.34.normed, f32[9,256]{1,0:T(8,128)S(1)} %bias.1, f32[1024,1152]{1,0:T(8,128)S(1)} %units_third.1.before, ...), custom_call_target="tpu_custom_call" | custom-call | tf_op jit(solution)/shard_map/finish_other/pallas_call | solution.py:441
  75.9 2.9 %collective-permute-start.18 = (f32[512,1152]{1,0:T(8,128)S(1)}, f32[512,1152]{1,0:T(8,128)S(1)}, u32[]{:S(2)}, u32[]{:S(2)}) collective-permute-start(f32[512,1152]{1,0:T(8,128)S(1)} %get-tuple-element.45), channel_id=1, source_target_pairs={{8,0},{9,1},{10,2},{11,3},{12,4},{13,5},{14,6},{15,7},{0,8},{1,9},... | collective-permute-start | bytes 7077896 | tf_op jit(solution)/shard_map/ppermute | solution.py:32
  78.8 4.3 %finish_own.1.here_part = f32[512,1152]{1,0:T(8,128)S(1)} custom-call(bf16[1024,1152]{1,0:T(8,128)(2,1)S(1)} %get-tuple-element.34.normed, f32[9,256]{1,0:T(8,128)S(1)} %bias.1, f32[1024,1152]{1,0:T(8,128)S(1)} %units_third.1.before, bf16[640,1152]{1,0:T(8,128)(2,1)S(1)} %get-tuple-element.43.up, bf16[640,1152]{1,0:T(8,128)(2,1)S(1)} %get-tuple-element.44.down, ...), custom_call_target="tpu_custom_call" | custom-call | tf_op jit(solution)/shard_map/finish_own/pallas_call | solution.py:450
  85.3 3.4 %collective-permute-start.19 = (bf16[32,1152]{1,0:T(8,128)(2,1)S(1)}, bf16[32,1152]{1,0:T(8,128)(2,1)S(1)}, u32[]{:S(2)}, u32[]{:S(2)}) collective-permute-start(bf16[32,1152]{1,0:T(8,128)(2,1)S(1)} %unit.1), channel_id=1, source_target_pairs={{1,0},{2,1},{3,2},{0,3},{5,4},{6,5},{7,6},{4,7},{9,8},{10,9},{11,1... | collective-permute-start | bytes 221192 | tf_op jit(solution)/shard_map/ppermute | solution.py:32
  99.3 3.1 %collective-permute-done.24 = bf16[32,1152]{1,0:T(8,128)(2,1)S(1)} collective-permute-done((bf16[32,1152]{1,0:T(8,128)(2,1)S(1)}, bf16[32,1152]{1,0:T(8,128)(2,1)S(1)}, u32[]{:S(2)}, u32[]{:S(2)}) %collective-permute-start.24) | collective-permute-done | bytes 73760 | tf_op jit(solution)/shard_map/ppermute | solution.py:32
  103.9 3.2 %collective-permute-done.26 = bf16[32,1152]{1,0:T(8,128)(2,1)S(1)} collective-permute-done((bf16[32,1152]{1,0:T(8,128)(2,1)S(1)}, bf16[32,1152]{1,0:T(8,128)(2,1)S(1)}, u32[]{:S(2)}, u32[]{:S(2)}) %collective-permute-start.26) | collective-permute-done | bytes 73760 | tf_op jit(solution)/shard_map/ppermute | solution.py:32
  107.0 2.4 %collective-permute-start.30 = (bf16[128,1152]{1,0:T(8,128)(2,1)S(1)}, bf16[128,1152]{1,0:T(8,128)(2,1)S(1)}, u32[]{:S(2)}, u32[]{:S(2)}) collective-permute-start(bf16[128,1152]{1,0:T(8,128)(2,1)S(1)} %constant_dynamic-update-slice_fusion.refs_2_), channel_id=1, source_target_pairs={{8,0},{9,1},{10,2},{11,3},{12,4},{13,5},{14,6},{15,7},{0,8},{1,9},... | collective-permute-start | bytes 884744 | tf_op jit(solution)/shard_map/ppermute | solution.py:32
  112.0 4.6 %collective-permute-done.32.far.refs_13_ = bf16[8,32,256]{2,1,0:T(8,128)(2,1)S(1)} collective-permute-done((bf16[8,32,256]{2,1,0:T(8,128)(2,1)S(1)}, bf16[8,32,256]{2,1,0:T(8,128)(2,1)S(1)}, u32[]{:S(2)}, u32[]{:S(2)}) %collective-permute-start.32) | collective-permute-done | bytes 131104 | tf_op jit(solution)/shard_map/ppermute | solution.py:32
  119.1 2.6 %scores.1 = (f32[32,1152]{1,0:T(8,128)S(1)}, bf16[32,1152]{1,0:T(8,128)(2,1)S(1)}, bf16[32,1152]{1,0:T(8,128)(2,1)S(1)}, bf16[32,1152]{1,0:T(8,128)(2,1)S(1)}) custom-call(f32[1]{0:T(128)} %copy.25.logit_scale, f32[1]{0:T(128)S(6)} %copy.26.logit_bias, bf16[128,1152]{1,0:T(8,128)(2,1)S(1)} %pad_maximum_fusion.refs_0_, ...), custom_call_target="tpu_custom_call" | custom-call | tf_op jit(solution)/shard_map/scores/pallas_call | solution.py:478
  126.8 5.0 %collective-permute-done.35 = bf16[32,1152]{1,0:T(8,128)(2,1)S(1)} collective-permute-done((bf16[32,1152]{1,0:T(8,128)(2,1)S(1)}, bf16[32,1152]{1,0:T(8,128)(2,1)S(1)}, u32[]{:S(2)}, u32[]{:S(2)}) %collective-permute-start.35) | collective-permute-done | bytes 73760 | tf_op jit(solution)/shard_map/ppermute | solution.py:32
  (100 shorter events, 39.9 us)
Async XLA Ops:
  3.5 14.6 %collective-permute-start = (bf16[512,1152]{1,0:T(8,128)(2,1)S(1)}, bf16[512,1152]{1,0:T(8,128)(2,1)S(1)}, u32[]{:S(2)}, u32[]{:S(2)}) collective-permute-start(bf16[512,1152]{1,0:T(8,128)(2,1)S(1)} %norm.1.own), channel_id=1, source_target_pairs={{8,0},{9,1},{10,2},{11,3},{12,4},{13,5},{14,6},{15,7},{0,8},{1,9},... | collective-permute-start | bytes 3538952 | tf_op jit(solution)/shard_map/ppermute | solution.py:32
  12.1 16.1 %collective-permute-start.1 = (bf16[272,1152]{1,0:T(8,128)(2,1)}, bf16[272,1152]{1,0:T(8,128)(2,1)}, u32[]{:S(2)}, u32[]{:S(2)}) collective-permute-start(bf16[272,1152]{1,0:T(8,128)(2,1)} %get-tuple-element.31.part_p), channel_id=1, source_target_pairs={{1,0},{2,1},{3,2},{0,3},{5,4},{6,5},{7,6},{4,7},{9,8},{10,9},{11,1... | collective-permute-start | bytes 1880072 | tf_op jit(solution)/shard_map/ppermute | solution.py:32
  14.6 19.4 %collective-permute-start.7 = (bf16[272,1152]{1,0:T(8,128)(2,1)S(1)}, bf16[272,1152]{1,0:T(8,128)(2,1)}, u32[]{:S(2)}, u32[]{:S(2)}) collective-permute-start(bf16[272,1152]{1,0:T(8,128)(2,1)S(1)} %get-tuple-element.33.part_q.refs_0_), channel_id=1, source_target_pairs={{20,0},{21,1},{22,2},{23,3},{0,4},{1,5},{2,6},{3,7},{28,8},{29,9},... | collective-permute-start | bytes 1880072 | tf_op jit(solution)/shard_map/ppermute | solution.py:32
  15.9 18.1 %collective-permute-start.2 = (bf16[272,1152]{1,0:T(8,128)(2,1)}, bf16[272,1152]{1,0:T(8,128)(2,1)}, u32[]{:S(2)}, u32[]{:S(2)}) collective-permute-start(bf16[272,1152]{1,0:T(8,128)(2,1)} %get-tuple-element.31.part_p), channel_id=1, source_target_pairs={{3,0},{0,1},{1,2},{2,3},{7,4},{4,5},{5,6},{6,7},{11,8},{8,9},{9,10... | collective-permute-start | bytes 1880072 | tf_op jit(solution)/shard_map/ppermute | solution.py:32
  15.9 18.1 %collective-permute-start.3 = (bf16[272,1152]{1,0:T(8,128)(2,1)}, bf16[272,1152]{1,0:T(8,128)(2,1)}, u32[]{:S(2)}, u32[]{:S(2)}) collective-permute-start(bf16[272,1152]{1,0:T(8,128)(2,1)} %get-tuple-element.31.part_p), channel_id=1, source_target_pairs={{4,0},{5,1},{6,2},{7,3},{16,4},{17,5},{18,6},{19,7},{12,8},{13,9},... | collective-permute-start | bytes 1880072 | tf_op jit(solution)/shard_map/ppermute | solution.py:32
  19.2 12.0 %collective-permute-start.6 = (bf16[32,1152]{1,0:T(8,128)(2,1)S(1)}, bf16[32,1152]{1,0:T(8,128)(2,1)S(1)}, u32[]{:S(2)}, u32[]{:S(2)}) collective-permute-start(bf16[32,1152]{1,0:T(8,128)(2,1)S(1)} %fusion.1.refs_8_), channel_id=1, source_target_pairs={{96,0},{97,1},{98,2},{99,3},{100,4},{101,5},{102,6},{103,7},{104,8... | collective-permute-start | bytes 221192 | tf_op jit(solution)/shard_map/ppermute | solution.py:32
  28.3 15.3 %collective-permute-start.10 = (bf16[272,1152]{1,0:T(8,128)(2,1)}, bf16[272,1152]{1,0:T(8,128)(2,1)S(1)}, u32[]{:S(2)}, u32[]{:S(2)}) collective-permute-start(bf16[272,1152]{1,0:T(8,128)(2,1)} %collective-permute-done.1.refs_1_), channel_id=1, source_target_pairs={{1,0},{2,1},{3,2},{0,3},{5,4},{6,5},{7,6},{4,7},{9,8},{10,9},{11,1... | collective-permute-start | bytes 1880072 | tf_op jit(solution)/shard_map/ppermute | solution.py:32
  31.2 14.8 %collective-permute-start.11 = (bf16[272,1152]{1,0:T(8,128)(2,1)}, bf16[272,1152]{1,0:T(8,128)(2,1)S(1)}, u32[]{:S(2)}, u32[]{:S(2)}) collective-permute-start(bf16[272,1152]{1,0:T(8,128)(2,1)} %collective-permute-done.1.refs_1_), channel_id=1, source_target_pairs={{4,0},{5,1},{6,2},{7,3},{16,4},{17,5},{18,6},{19,7},{12,8},{13,9},... | collective-permute-start | bytes 1880072 | tf_op jit(solution)/shard_map/ppermute | solution.py:32
  34.0 15.1 %collective-permute-start.12 = (bf16[272,1152]{1,0:T(8,128)(2,1)}, bf16[272,1152]{1,0:T(8,128)(2,1)S(1)}, u32[]{:S(2)}, u32[]{:S(2)}) collective-permute-start(bf16[272,1152]{1,0:T(8,128)(2,1)} %collective-permute-done.7.refs_4_.refs_0_), channel_id=1, source_target_pairs={{3,0},{0,1},{1,2},{2,3},{7,4},{4,5},{5,6},{6,7},{11,8},{8,9},{9,10... | collective-permute-start | bytes 1880072 | tf_op jit(solution)/shard_map/ppermute | solution.py:32
  34.0 16.3 %collective-permute-start.13 = (bf16[272,1152]{1,0:T(8,128)(2,1)}, bf16[272,1152]{1,0:T(8,128)(2,1)S(1)}, u32[]{:S(2)}, u32[]{:S(2)}) collective-permute-start(bf16[272,1152]{1,0:T(8,128)(2,1)} %collective-permute-done.2.refs_2_), channel_id=1, source_target_pairs={{20,0},{21,1},{22,2},{23,3},{0,4},{1,5},{2,6},{3,7},{28,8},{29,9},... | collective-permute-start | bytes 1880072 | tf_op jit(solution)/shard_map/ppermute | solution.py:32
  34.1 18.1 %collective-permute-start.9 = (bf16[272,1152]{1,0:T(8,128)(2,1)}, bf16[272,1152]{1,0:T(8,128)(2,1)S(1)}, u32[]{:S(2)}, u32[]{:S(2)}) collective-permute-start(bf16[272,1152]{1,0:T(8,128)(2,1)} %collective-permute-done.2.refs_2_), channel_id=1, source_target_pairs={{224,0},{225,1},{226,2},{227,3},{228,4},{229,5},{230,6},{231,7},{2... | collective-permute-start | bytes 1880072 | tf_op jit(solution)/shard_map/ppermute | solution.py:32
  43.6 14.7 %collective-permute-start.8 = (bf16[272,1152]{1,0:T(8,128)(2,1)}, bf16[272,1152]{1,0:T(8,128)(2,1)S(1)}, u32[]{:S(2)}, u32[]{:S(2)}) collective-permute-start(bf16[272,1152]{1,0:T(8,128)(2,1)} %collective-permute-done.1.refs_1_), channel_id=1, source_target_pairs={{32,0},{33,1},{34,2},{35,3},{36,4},{37,5},{38,6},{39,7},{40,8},{41... | collective-permute-start | bytes 1880072 | tf_op jit(solution)/shard_map/ppermute | solution.py:32
  49.1 22.6 %collective-permute-start.15 = (bf16[272,1152]{1,0:T(8,128)(2,1)S(1)}, bf16[272,1152]{1,0:T(8,128)(2,1)S(1)}, u32[]{:S(2)}, u32[]{:S(2)}) collective-permute-start(bf16[272,1152]{1,0:T(8,128)(2,1)S(1)} %collective-permute-done.10.refs_5_), channel_id=1, source_target_pairs={{224,0},{225,1},{226,2},{227,3},{228,4},{229,5},{230,6},{231,7},{2... | collective-permute-start | bytes 1880072 | tf_op jit(solution)/shard_map/ppermute | solution.py:32
  49.8 21.9 %collective-permute-start.16 = (bf16[272,1152]{1,0:T(8,128)(2,1)S(1)}, bf16[272,1152]{1,0:T(8,128)(2,1)S(1)}, u32[]{:S(2)}, u32[]{:S(2)}) collective-permute-start(bf16[272,1152]{1,0:T(8,128)(2,1)S(1)} %collective-permute-done.10.refs_5_), channel_id=1, source_target_pairs={{4,0},{5,1},{6,2},{7,3},{16,4},{17,5},{18,6},{19,7},{12,8},{13,9},... | collective-permute-start | bytes 1880072 | tf_op jit(solution)/shard_map/ppermute | solution.py:32
  50.3 21.4 %collective-permute-start.14 = (bf16[272,1152]{1,0:T(8,128)(2,1)S(1)}, bf16[272,1152]{1,0:T(8,128)(2,1)S(1)}, u32[]{:S(2)}, u32[]{:S(2)}) collective-permute-start(bf16[272,1152]{1,0:T(8,128)(2,1)S(1)} %collective-permute-done.11.refs_3_), channel_id=1, source_target_pairs={{32,0},{33,1},{34,2},{35,3},{36,4},{37,5},{38,6},{39,7},{40,8},{41... | collective-permute-start | bytes 1880072 | tf_op jit(solution)/shard_map/ppermute | solution.py:32
  52.2 19.5 %collective-permute-start.17 = (bf16[272,1152]{1,0:T(8,128)(2,1)S(1)}, bf16[272,1152]{1,0:T(8,128)(2,1)S(1)}, u32[]{:S(2)}, u32[]{:S(2)}) collective-permute-start(bf16[272,1152]{1,0:T(8,128)(2,1)S(1)} %collective-permute-done.12.refs_6_.refs_0_), channel_id=1, source_target_pairs={{3,0},{0,1},{1,2},{2,3},{7,4},{4,5},{5,6},{6,7},{11,8},{8,9},{9,10... | collective-permute-start | bytes 1880072 | tf_op jit(solution)/shard_map/ppermute | solution.py:32
  89.4 9.2 %collective-permute-start.23 = (bf16[32,1152]{1,0:T(8,128)(2,1)S(1)}, bf16[32,1152]{1,0:T(8,128)(2,1)S(1)}, u32[]{:S(2)}, u32[]{:S(2)}) collective-permute-start(bf16[32,1152]{1,0:T(8,128)(2,1)S(1)} %unit.1), channel_id=1, source_target_pairs={{16,0},{17,1},{18,2},{19,3},{20,4},{21,5},{22,6},{23,7},{24,8},{25... | collective-permute-start | bytes 221192 | tf_op jit(solution)/shard_map/ppermute | solution.py:32
  95.4 14.0 %collective-permute-start.22 = (bf16[128,1152]{1,0:T(8,128)(2,1)S(1)}, bf16[128,1152]{1,0:T(8,128)(2,1)S(1)}, u32[]{:S(2)}, u32[]{:S(2)}) collective-permute-start(bf16[128,1152]{1,0:T(8,128)(2,1)S(1)} %pad_maximum_fusion.refs_0_), channel_id=1, source_target_pairs={{4,0},{5,1},{6,2},{7,3},{16,4},{17,5},{18,6},{19,7},{12,8},{13,9},... | collective-permute-start | bytes 884744 | tf_op jit(solution)/shard_map/ppermute | solution.py:32
  97.5 12.1 %collective-permute-start.27 = (bf16[128,1152]{1,0:T(8,128)(2,1)S(1)}, bf16[128,1152]{1,0:T(8,128)(2,1)S(1)}, u32[]{:S(2)}, u32[]{:S(2)}) collective-permute-start(bf16[128,1152]{1,0:T(8,128)(2,1)S(1)} %pad_maximum_fusion.refs_0_), channel_id=1, source_target_pairs={{20,0},{21,1},{22,2},{23,3},{0,4},{1,5},{2,6},{3,7},{28,8},{29,9},... | collective-permute-start | bytes 884744 | tf_op jit(solution)/shard_map/ppermute | solution.py:32
  97.5 21.5 %collective-permute-start.28 = (bf16[128,1152]{1,0:T(8,128)(2,1)S(1)}, bf16[128,1152]{1,0:T(8,128)(2,1)S(1)}, u32[]{:S(2)}, u32[]{:S(2)}) collective-permute-start(bf16[128,1152]{1,0:T(8,128)(2,1)S(1)} %pad_maximum_fusion.refs_0_), channel_id=1, source_target_pairs={{8,0},{9,1},{10,2},{11,3},{12,4},{13,5},{14,6},{15,7},{0,8},{1,9},... | collective-permute-start | bytes 884744 | tf_op jit(solution)/shard_map/ppermute | solution.py:32
  107.0 12.0 %collective-permute-start.30 = (bf16[128,1152]{1,0:T(8,128)(2,1)S(1)}, bf16[128,1152]{1,0:T(8,128)(2,1)S(1)}, u32[]{:S(2)}, u32[]{:S(2)}) collective-permute-start(bf16[128,1152]{1,0:T(8,128)(2,1)S(1)} %constant_dynamic-update-slice_fusion.refs_2_), channel_id=1, source_target_pairs={{8,0},{9,1},{10,2},{11,3},{12,4},{13,5},{14,6},{15,7},{0,8},{1,9},... | collective-permute-start | bytes 884744 | tf_op jit(solution)/shard_map/ppermute | solution.py:32
  109.5 9.6 %collective-permute-start.29 = (bf16[128,1152]{1,0:T(8,128)(2,1)S(1)}, bf16[128,1152]{1,0:T(8,128)(2,1)S(1)}, u32[]{:S(2)}, u32[]{:S(2)}) collective-permute-start(bf16[128,1152]{1,0:T(8,128)(2,1)S(1)} %collective-permute-done.22.refs_1_), channel_id=1, source_target_pairs={{8,0},{9,1},{10,2},{11,3},{12,4},{13,5},{14,6},{15,7},{0,8},{1,9},... | collective-permute-start | bytes 884744 | tf_op jit(solution)/shard_map/ppermute | solution.py:32
  109.6 9.5 %collective-permute-start.31 = (bf16[128,1152]{1,0:T(8,128)(2,1)S(1)}, bf16[128,1152]{1,0:T(8,128)(2,1)S(1)}, u32[]{:S(2)}, u32[]{:S(2)}) collective-permute-start(bf16[128,1152]{1,0:T(8,128)(2,1)S(1)} %collective-permute-done.27.refs_3_), channel_id=1, source_target_pairs={{8,0},{9,1},{10,2},{11,3},{12,4},{13,5},{14,6},{15,7},{0,8},{1,9},... | collective-permute-start | bytes 884744 | tf_op jit(solution)/shard_map/ppermute | solution.py:32
  124.0 9.7 %collective-permute-start.36 = (bf16[32,1152]{1,0:T(8,128)(2,1)S(1)}, bf16[32,1152]{1,0:T(8,128)(2,1)S(1)}, u32[]{:S(2)}, u32[]{:S(2)}) collective-permute-start(bf16[32,1152]{1,0:T(8,128)(2,1)S(1)} %get-tuple-element.56), channel_id=1, source_target_pairs={{160,0},{161,1},{162,2},{163,3},{164,4},{165,5},{166,6},{167,7},{1... | collective-permute-start | bytes 221192 | tf_op jit(solution)/shard_map/ppermute | solution.py:32
  (27 other events, 189.2 us)

commit v3 on v2

--- a/solution.py
+++ b/solution.py
@@ -384,6 +384,13 @@
     ).astype(jnp.bfloat16)
     pictures = [image_unit] + [come_from(image_unit, dz=d) for d in (1, 2, 3)]
 
+    tiles = jnp.transpose(after(teacher_logits, normed), (1, 2, 0))
+    kinds = [pltpu.VMEM((n, *tiles.shape[1:]), tiles.dtype) for n in (4, 4, 8)]
+    tiles_own, tiles_near, tiles_far = kernel_of(tile_kernel, 4)(
+        out_shape=tuple(kinds), in_specs=[VMEM], out_specs=(VMEM,) * 3, name="tiles"
+    )(tiles)
+    tiles_far = come_from(tiles_far, dy=2)
+
     def scratch(first, last):
         return [pltpu.VMEM((last - first, width), jnp.bfloat16)] * 2
 
@@ -416,7 +423,7 @@
     left_q = come_from(left_p, dz=-1)
     flip_left_p = come_from(left_p, dy=-1)
     parts = (own_p, own_q, right_p, left_p, flip_p, flip_q)
-    total = add_units(TILE, 768, total, parts, "units_second")
+    total = add_units(TILE, 2 * TILE, total, parts, "units_second")
 
     over_p, flip_right_p, flip_left_q = after((over_p, flip_right_p, flip_left_q), total)
     flip_over_q = come_from(flip_left_q, dx=-1)
@@ -424,15 +431,8 @@
     over_q = come_from(over_p, dz=-1)
     flip_over_p = come_from(over_p, dy=1)
 
-    tiles = jnp.transpose(after(teacher_logits, total), (1, 2, 0))
-    kinds = [pltpu.VMEM((n, *tiles.shape[1:]), tiles.dtype) for n in (4, 4, 8)]
-    tiles_own, tiles_near, tiles_far = kernel_of(tile_kernel, 4)(
-        out_shape=tuple(kinds), in_specs=[VMEM], out_specs=(VMEM,) * 3, name="tiles"
-    )(tiles)
-    tiles_far = come_from(tiles_far, dy=2)
-
     parts = parts + (right_q, left_q, flip_right_p, flip_left_p, over_p, flip_left_q)
-    total = add_units(768, 1536, total, parts, "units_third")
+    total = add_units(2 * TILE, 1536, total, parts, "units_third")
 
     first, last = 1536, units
     parts = (parts + (flip_right_q, over_q, flip_over_p, flip_over_q))[first // PART :]

time: 136 us -> 138 us (1.015)
  starting transfers between devices: 51.9 us -> 54.5 us
    ppermute x37, starting transfers between devices: 51.9 us -> 54.5 us  [come_from(): return lax.ppermute(array, AXES, pairs)]
  transfers between devices with their start and end apart: 37 -> 37, of which waited for: 15 -> 14; matrix products, arithmetic and copies ran while one was open for 0% -> 0% of each run, Pallas kernels for 21% -> 21%
where the time goes in v3:
time: 138 us; the launch traced here: 136 us
  starting transfers between devices  54.5 us (39%)
  Pallas kernels  40.5 us (29%)
  waiting for transfers between devices  36.2 us (26%)
  local copies, waits for them, and re-layouts  2.51 us (2%)
  between operations  1.63 us (1%)
    ppermute x37, starting transfers between devices, come_from(): return lax.ppermute(array, AXES, pairs)  54.5 us
    ppermute x37, waiting for transfers between devices, come_from(): return lax.ppermute(array, AXES, pairs)  36.2 us
    pallas_call x2, Pallas kernels, add_units(): kernel_of(functools.partial(add_kernel, first, last, len(parts)))  18.3 us
    pallas_call x1, Pallas kernels, on_device(): kernel_of(functools.partial(first_kernel, TILE))  5.13 us
    pallas_call x1, Pallas kernels, on_device(): kernel_of(functools.partial(finish_own_kernel, first, last))  4.29 us
    pallas_call x1, Pallas kernels, on_device(): kernel_of(functools.partial(finish_other_kernel, first, last, len(parts)))  4.18 us
  transfers between devices with their start and end apart: 37, of which 14 were waited for; matrix products, arithmetic and copies ran while one was open for 0% of the time, Pallas kernels for 21%

profile of v3, /device:TPU:1, one launch (start us, length us, event | category | flops | bytes accessed | tf_op | source)
XLA Modules:
  0.0 136.2 jit_solution(7840452437510831968)
XLA Ops:
  3.5 3.3 %collective-permute-start = (bf16[512,1152]{1,0:T(8,128)(2,1)S(1)}, bf16[512,1152]{1,0:T(8,128)(2,1)S(1)}, u32[]{:S(2)}, u32[]{:S(2)}) collective-permute-start(bf16[512,1152]{1,0:T(8,128)(2,1)S(1)} %norm.1.own), channel_id=1, source_target_pairs={{8,0},{9,1},{10,2},{11,3},{12,4},{13,5},{14,6},{15,7},{0,8},{1,9},... | collective-permute-start | bytes 3538952 | tf_op jit(solution)/shard_map/ppermute | solution.py:32
  7.0 4.0 %collective-permute-start.4 = (bf16[32,1152]{1,0:T(8,128)(2,1)S(1)}, bf16[32,1152]{1,0:T(8,128)(2,1)S(1)}, u32[]{:S(2)}, u32[]{:S(2)}) collective-permute-start(bf16[32,1152]{1,0:T(8,128)(2,1)S(1)} %fusion.1.refs_8_), channel_id=1, source_target_pairs={{32,0},{33,1},{34,2},{35,3},{36,4},{37,5},{38,6},{39,7},{40,8},{41... | collective-permute-start | bytes 221192 | tf_op jit(solution)/shard_map/ppermute | solution.py:32
  12.1 2.5 %collective-permute-start.1 = (bf16[272,1152]{1,0:T(8,128)(2,1)}, bf16[272,1152]{1,0:T(8,128)(2,1)}, u32[]{:S(2)}, u32[]{:S(2)}) collective-permute-start(bf16[272,1152]{1,0:T(8,128)(2,1)} %get-tuple-element.31.part_p), channel_id=1, source_target_pairs={{1,0},{2,1},{3,2},{0,3},{5,4},{6,5},{7,6},{4,7},{9,8},{10,9},{11,1... | collective-permute-start | bytes 1880072 | tf_op jit(solution)/shard_map/ppermute | solution.py:32
  23.2 5.1 %units_first.1 = (bf16[1024,1152]{1,0:T(8,128)(2,1)S(1)}, f32[1024,1152]{1,0:T(8,128)S(1)}, f32[32,16]{1,0:T(8,128)S(1)}) custom-call(bf16[512,1152]{1,0:T(8,128)(2,1)S(1)} %norm.1.own, bf16[512,1152]{1,0:T(8,128)(2,1)S(1)} %copy-done.3, f32[9,256]{1,0:T(8,128)S(1)} %bias.1, s32[32,16]{1,0:T(8,128)S(1)} %copy.19.ids, ...), custom_call_target="tpu_custom_call" | custom-call | tf_op jit(solution)/shard_map/units_first/pallas_call | solution.py:398
  28.3 2.9 %collective-permute-start.10 = (bf16[272,1152]{1,0:T(8,128)(2,1)}, bf16[272,1152]{1,0:T(8,128)(2,1)S(1)}, u32[]{:S(2)}, u32[]{:S(2)}) collective-permute-start(bf16[272,1152]{1,0:T(8,128)(2,1)} %collective-permute-done.1.refs_1_), channel_id=1, source_target_pairs={{1,0},{2,1},{3,2},{0,3},{5,4},{6,5},{7,6},{4,7},{9,8},{10,9},{11,1... | collective-permute-start | bytes 1880072 | tf_op jit(solution)/shard_map/ppermute | solution.py:32
  31.3 2.7 %collective-permute-start.11 = (bf16[272,1152]{1,0:T(8,128)(2,1)}, bf16[272,1152]{1,0:T(8,128)(2,1)S(1)}, u32[]{:S(2)}, u32[]{:S(2)}) collective-permute-start(bf16[272,1152]{1,0:T(8,128)(2,1)} %collective-permute-done.1.refs_1_), channel_id=1, source_target_pairs={{4,0},{5,1},{6,2},{7,3},{16,4},{17,5},{18,6},{19,7},{12,8},{13,9},... | collective-permute-start | bytes 1880072 | tf_op jit(solution)/shard_map/ppermute | solution.py:32
  34.9 5.3 %units_second.1.before = f32[1024,1152]{1,0:T(8,128)S(1)} custom-call(bf16[1024,1152]{1,0:T(8,128)(2,1)S(1)} %get-tuple-element.34.normed, f32[9,256]{1,0:T(8,128)S(1)} %bias.1, f32[1024,1152]{1,0:T(8,128)S(1)} %get-tuple-element.35.before, bf16[272,1152]{1,0:T(8,128)(2,1)S(1)} %get-tuple-element.33.part_q.refs_0_, ...), custom_call_target="tpu_custom_call", output_to_operand_aliasing={{}: (2, {})} | custom-call | tf_op jit(solution)/shard_map/units_second/pallas_call | solution.py:412
  40.3 3.3 %collective-permute-done.10.refs_7_ = bf16[272,1152]{1,0:T(8,128)(2,1)S(1)} collective-permute-done((bf16[272,1152]{1,0:T(8,128)(2,1)}, bf16[272,1152]{1,0:T(8,128)(2,1)S(1)}, u32[]{:S(2)}, u32[]{:S(2)}) %collective-permute-start.10) | collective-permute-done | bytes 626720 | tf_op jit(solution)/shard_map/ppermute | solution.py:32
  46.1 3.0 %collective-permute-done.12.refs_8_.refs_0_ = bf16[272,1152]{1,0:T(8,128)(2,1)S(1)} collective-permute-done((bf16[272,1152]{1,0:T(8,128)(2,1)}, bf16[272,1152]{1,0:T(8,128)(2,1)S(1)}, u32[]{:S(2)}, u32[]{:S(2)}) %collective-permute-start.12) | collective-permute-done | bytes 626720 | tf_op jit(solution)/shard_map/ppermute | solution.py:32
  52.7 5.6 %collective-permute-done.8.refs_3_ = bf16[272,1152]{1,0:T(8,128)(2,1)S(1)} collective-permute-done((bf16[272,1152]{1,0:T(8,128)(2,1)}, bf16[272,1152]{1,0:T(8,128)(2,1)S(1)}, u32[]{:S(2)}, u32[]{:S(2)}) %collective-permute-start.8) | collective-permute-done | bytes 626720 | tf_op jit(solution)/shard_map/ppermute | solution.py:32
  58.3 13.0 %units_third.1.before = f32[1024,1152]{1,0:T(8,128)S(1)} custom-call(bf16[1024,1152]{1,0:T(8,128)(2,1)S(1)} %get-tuple-element.34.normed, f32[9,256]{1,0:T(8,128)S(1)} %bias.1, f32[1024,1152]{1,0:T(8,128)S(1)} %units_second.1.before, bf16[272,1152]{1,0:T(8,128)(2,1)} %collective-permute-done.2.refs_2_.refs_0_, ...), custom_call_target="tpu_custom_call", output_to_operand_aliasing={{}: (2, {})} | custom-call | tf_op jit(solution)/shard_map/units_third/pallas_call | solution.py:412
  71.7 4.2 %finish_other.1 = (f32[512,1152]{1,0:T(8,128)S(1)}, bf16[640,1152]{1,0:T(8,128)(2,1)S(1)}, bf16[640,1152]{1,0:T(8,128)(2,1)S(1)}) custom-call(bf16[1024,1152]{1,0:T(8,128)(2,1)S(1)} %get-tuple-element.34.normed, f32[9,256]{1,0:T(8,128)S(1)} %bias.1, f32[1024,1152]{1,0:T(8,128)S(1)} %units_third.1.before, ...), custom_call_target="tpu_custom_call" | custom-call | tf_op jit(solution)/shard_map/finish_other/pallas_call | solution.py:441
  75.9 4.9 %collective-permute-start.18 = (f32[512,1152]{1,0:T(8,128)S(1)}, f32[512,1152]{1,0:T(8,128)S(1)}, u32[]{:S(2)}, u32[]{:S(2)}) collective-permute-start(f32[512,1152]{1,0:T(8,128)S(1)} %get-tuple-element.45), channel_id=1, source_target_pairs={{8,0},{9,1},{10,2},{11,3},{12,4},{13,5},{14,6},{15,7},{0,8},{1,9},... | collective-permute-start | bytes 7077896 | tf_op jit(solution)/shard_map/ppermute | solution.py:32
  80.8 4.3 %finish_own.1.here_part = f32[512,1152]{1,0:T(8,128)S(1)} custom-call(bf16[1024,1152]{1,0:T(8,128)(2,1)S(1)} %get-tuple-element.34.normed, f32[9,256]{1,0:T(8,128)S(1)} %bias.1, f32[1024,1152]{1,0:T(8,128)S(1)} %units_third.1.before, bf16[640,1152]{1,0:T(8,128)(2,1)S(1)} %get-tuple-element.43.up, bf16[640,1152]{1,0:T(8,128)(2,1)S(1)} %get-tuple-element.44.down, ...), custom_call_target="tpu_custom_call" | custom-call | tf_op jit(solution)/shard_map/finish_own/pallas_call | solution.py:450
  87.3 3.4 %collective-permute-start.19 = (bf16[32,1152]{1,0:T(8,128)(2,1)S(1)}, bf16[32,1152]{1,0:T(8,128)(2,1)S(1)}, u32[]{:S(2)}, u32[]{:S(2)}) collective-permute-start(bf16[32,1152]{1,0:T(8,128)(2,1)S(1)} %unit.1), channel_id=1, source_target_pairs={{1,0},{2,1},{3,2},{0,3},{5,4},{6,5},{7,6},{4,7},{9,8},{10,9},{11,1... | collective-permute-start | bytes 221192 | tf_op jit(solution)/shard_map/ppermute | solution.py:32
  91.4 2.5 %collective-permute-start.23 = (bf16[32,1152]{1,0:T(8,128)(2,1)S(1)}, bf16[32,1152]{1,0:T(8,128)(2,1)S(1)}, u32[]{:S(2)}, u32[]{:S(2)}) collective-permute-start(bf16[32,1152]{1,0:T(8,128)(2,1)S(1)} %unit.1), channel_id=1, source_target_pairs={{16,0},{17,1},{18,2},{19,3},{20,4},{21,5},{22,6},{23,7},{24,8},{25... | collective-permute-start | bytes 221192 | tf_op jit(solution)/shard_map/ppermute | solution.py:32
  97.4 2.4 %collective-permute-start.22 = (bf16[128,1152]{1,0:T(8,128)(2,1)S(1)}, bf16[128,1152]{1,0:T(8,128)(2,1)S(1)}, u32[]{:S(2)}, u32[]{:S(2)}) collective-permute-start(bf16[128,1152]{1,0:T(8,128)(2,1)S(1)} %pad_maximum_fusion.refs_0_), channel_id=1, source_target_pairs={{4,0},{5,1},{6,2},{7,3},{16,4},{17,5},{18,6},{19,7},{12,8},{13,9},... | collective-permute-start | bytes 884744 | tf_op jit(solution)/shard_map/ppermute | solution.py:32
  101.6 3.1 %collective-permute-done.24 = bf16[32,1152]{1,0:T(8,128)(2,1)S(1)} collective-permute-done((bf16[32,1152]{1,0:T(8,128)(2,1)S(1)}, bf16[32,1152]{1,0:T(8,128)(2,1)S(1)}, u32[]{:S(2)}, u32[]{:S(2)}) %collective-permute-start.24) | collective-permute-done | bytes 73760 | tf_op jit(solution)/shard_map/ppermute | solution.py:32
  106.2 3.2 %collective-permute-done.26 = bf16[32,1152]{1,0:T(8,128)(2,1)S(1)} collective-permute-done((bf16[32,1152]{1,0:T(8,128)(2,1)S(1)}, bf16[32,1152]{1,0:T(8,128)(2,1)S(1)}, u32[]{:S(2)}, u32[]{:S(2)}) %collective-permute-start.26) | collective-permute-done | bytes 73760 | tf_op jit(solution)/shard_map/ppermute | solution.py:32
  109.4 2.4 %collective-permute-start.30 = (bf16[128,1152]{1,0:T(8,128)(2,1)S(1)}, bf16[128,1152]{1,0:T(8,128)(2,1)S(1)}, u32[]{:S(2)}, u32[]{:S(2)}) collective-permute-start(bf16[128,1152]{1,0:T(8,128)(2,1)S(1)} %constant_dynamic-update-slice_fusion.refs_2_), channel_id=1, source_target_pairs={{8,0},{9,1},{10,2},{11,3},{12,4},{13,5},{14,6},{15,7},{0,8},{1,9},... | collective-permute-start | bytes 884744 | tf_op jit(solution)/shard_map/ppermute | solution.py:32
  114.4 4.6 %collective-permute-done.32.far.refs_13_ = bf16[8,32,256]{2,1,0:T(8,128)(2,1)S(1)} collective-permute-done((bf16[8,32,256]{2,1,0:T(8,128)(2,1)S(1)}, bf16[8,32,256]{2,1,0:T(8,128)(2,1)S(1)}, u32[]{:S(2)}, u32[]{:S(2)}) %collective-permute-start.32) | collective-permute-done | bytes 131104 | tf_op jit(solution)/shard_map/ppermute | solution.py:32
  121.4 2.6 %scores.1 = (f32[32,1152]{1,0:T(8,128)S(1)}, bf16[32,1152]{1,0:T(8,128)(2,1)S(1)}, bf16[32,1152]{1,0:T(8,128)(2,1)S(1)}, bf16[32,1152]{1,0:T(8,128)(2,1)S(1)}) custom-call(f32[1]{0:T(128)} %copy.25.logit_scale, f32[1]{0:T(128)S(6)} %copy.26.logit_bias, bf16[128,1152]{1,0:T(8,128)(2,1)S(1)} %pad_maximum_fusion.refs_0_, ...), custom_call_target="tpu_custom_call" | custom-call | tf_op jit(solution)/shard_map/scores/pallas_call | solution.py:478
  129.2 3.9 %collective-permute-done.35 = bf16[32,1152]{1,0:T(8,128)(2,1)S(1)} collective-permute-done((bf16[32,1152]{1,0:T(8,128)(2,1)S(1)}, bf16[32,1152]{1,0:T(8,128)(2,1)S(1)}, u32[]{:S(2)}, u32[]{:S(2)}) %collective-permute-start.35) | collective-permute-done | bytes 73760 | tf_op jit(solution)/shard_map/ppermute | solution.py:32
  133.0 2.5 %collective-permute-done.36 = bf16[32,1152]{1,0:T(8,128)(2,1)S(1)} collective-permute-done((bf16[32,1152]{1,0:T(8,128)(2,1)S(1)}, bf16[32,1152]{1,0:T(8,128)(2,1)S(1)}, u32[]{:S(2)}, u32[]{:S(2)}) %collective-permute-start.36) | collective-permute-done | bytes 73760 | tf_op jit(solution)/shard_map/ppermute | solution.py:32
  (100 shorter events, 39.9 us)
Async XLA Ops:
  3.5 14.6 %collective-permute-start = (bf16[512,1152]{1,0:T(8,128)(2,1)S(1)}, bf16[512,1152]{1,0:T(8,128)(2,1)S(1)}, u32[]{:S(2)}, u32[]{:S(2)}) collective-permute-start(bf16[512,1152]{1,0:T(8,128)(2,1)S(1)} %norm.1.own), channel_id=1, source_target_pairs={{8,0},{9,1},{10,2},{11,3},{12,4},{13,5},{14,6},{15,7},{0,8},{1,9},... | collective-permute-start | bytes 3538952 | tf_op jit(solution)/shard_map/ppermute | solution.py:32
  12.1 16.1 %collective-permute-start.1 = (bf16[272,1152]{1,0:T(8,128)(2,1)}, bf16[272,1152]{1,0:T(8,128)(2,1)}, u32[]{:S(2)}, u32[]{:S(2)}) collective-permute-start(bf16[272,1152]{1,0:T(8,128)(2,1)} %get-tuple-element.31.part_p), channel_id=1, source_target_pairs={{1,0},{2,1},{3,2},{0,3},{5,4},{6,5},{7,6},{4,7},{9,8},{10,9},{11,1... | collective-permute-start | bytes 1880072 | tf_op jit(solution)/shard_map/ppermute | solution.py:32
  14.6 19.4 %collective-permute-start.7 = (bf16[272,1152]{1,0:T(8,128)(2,1)S(1)}, bf16[272,1152]{1,0:T(8,128)(2,1)}, u32[]{:S(2)}, u32[]{:S(2)}) collective-permute-start(bf16[272,1152]{1,0:T(8,128)(2,1)S(1)} %get-tuple-element.33.part_q.refs_0_), channel_id=1, source_target_pairs={{20,0},{21,1},{22,2},{23,3},{0,4},{1,5},{2,6},{3,7},{28,8},{29,9},... | collective-permute-start | bytes 1880072 | tf_op jit(solution)/shard_map/ppermute | solution.py:32
  15.9 18.1 %collective-permute-start.2 = (bf16[272,1152]{1,0:T(8,128)(2,1)}, bf16[272,1152]{1,0:T(8,128)(2,1)}, u32[]{:S(2)}, u32[]{:S(2)}) collective-permute-start(bf16[272,1152]{1,0:T(8,128)(2,1)} %get-tuple-element.31.part_p), channel_id=1, source_target_pairs={{3,0},{0,1},{1,2},{2,3},{7,4},{4,5},{5,6},{6,7},{11,8},{8,9},{9,10... | collective-permute-start | bytes 1880072 | tf_op jit(solution)/shard_map/ppermute | solution.py:32
  15.9 18.1 %collective-permute-start.3 = (bf16[272,1152]{1,0:T(8,128)(2,1)}, bf16[272,1152]{1,0:T(8,128)(2,1)}, u32[]{:S(2)}, u32[]{:S(2)}) collective-permute-start(bf16[272,1152]{1,0:T(8,128)(2,1)} %get-tuple-element.31.part_p), channel_id=1, source_target_pairs={{4,0},{5,1},{6,2},{7,3},{16,4},{17,5},{18,6},{19,7},{12,8},{13,9},... | collective-permute-start | bytes 1880072 | tf_op jit(solution)/shard_map/ppermute | solution.py:32
  19.2 12.0 %collective-permute-start.6 = (bf16[32,1152]{1,0:T(8,128)(2,1)S(1)}, bf16[32,1152]{1,0:T(8,128)(2,1)S(1)}, u32[]{:S(2)}, u32[]{:S(2)}) collective-permute-start(bf16[32,1152]{1,0:T(8,128)(2,1)S(1)} %fusion.1.refs_8_), channel_id=1, source_target_pairs={{96,0},{97,1},{98,2},{99,3},{100,4},{101,5},{102,6},{103,7},{104,8... | collective-permute-start | bytes 221192 | tf_op jit(solution)/shard_map/ppermute | solution.py:32
  28.3 15.3 %collective-permute-start.10 = (bf16[272,1152]{1,0:T(8,128)(2,1)}, bf16[272,1152]{1,0:T(8,128)(2,1)S(1)}, u32[]{:S(2)}, u32[]{:S(2)}) collective-permute-start(bf16[272,1152]{1,0:T(8,128)(2,1)} %collective-permute-done.1.refs_1_), channel_id=1, source_target_pairs={{1,0},{2,1},{3,2},{0,3},{5,4},{6,5},{7,6},{4,7},{9,8},{10,9},{11,1... | collective-permute-start | bytes 1880072 | tf_op jit(solution)/shard_map/ppermute | solution.py:32
  31.3 14.8 %collective-permute-start.11 = (bf16[272,1152]{1,0:T(8,128)(2,1)}, bf16[272,1152]{1,0:T(8,128)(2,1)S(1)}, u32[]{:S(2)}, u32[]{:S(2)}) collective-permute-start(bf16[272,1152]{1,0:T(8,128)(2,1)} %collective-permute-done.1.refs_1_), channel_id=1, source_target_pairs={{4,0},{5,1},{6,2},{7,3},{16,4},{17,5},{18,6},{19,7},{12,8},{13,9},... | collective-permute-start | bytes 1880072 | tf_op jit(solution)/shard_map/ppermute | solution.py:32
  34.0 15.1 %collective-permute-start.12 = (bf16[272,1152]{1,0:T(8,128)(2,1)}, bf16[272,1152]{1,0:T(8,128)(2,1)S(1)}, u32[]{:S(2)}, u32[]{:S(2)}) collective-permute-start(bf16[272,1152]{1,0:T(8,128)(2,1)} %collective-permute-done.7.refs_2_), channel_id=1, source_target_pairs={{3,0},{0,1},{1,2},{2,3},{7,4},{4,5},{5,6},{6,7},{11,8},{8,9},{9,10... | collective-permute-start | bytes 1880072 | tf_op jit(solution)/shard_map/ppermute | solution.py:32
  34.0 16.3 %collective-permute-start.13 = (bf16[272,1152]{1,0:T(8,128)(2,1)}, bf16[272,1152]{1,0:T(8,128)(2,1)S(1)}, u32[]{:S(2)}, u32[]{:S(2)}) collective-permute-start(bf16[272,1152]{1,0:T(8,128)(2,1)} %collective-permute-done.2.refs_2_.refs_0_), channel_id=1, source_target_pairs={{20,0},{21,1},{22,2},{23,3},{0,4},{1,5},{2,6},{3,7},{28,8},{29,9},... | collective-permute-start | bytes 1880072 | tf_op jit(solution)/shard_map/ppermute | solution.py:32
  34.1 18.1 %collective-permute-start.9 = (bf16[272,1152]{1,0:T(8,128)(2,1)}, bf16[272,1152]{1,0:T(8,128)(2,1)S(1)}, u32[]{:S(2)}, u32[]{:S(2)}) collective-permute-start(bf16[272,1152]{1,0:T(8,128)(2,1)} %collective-permute-done.2.refs_2_.refs_0_), channel_id=1, source_target_pairs={{224,0},{225,1},{226,2},{227,3},{228,4},{229,5},{230,6},{231,7},{2... | collective-permute-start | bytes 1880072 | tf_op jit(solution)/shard_map/ppermute | solution.py:32
  43.6 14.7 %collective-permute-start.8 = (bf16[272,1152]{1,0:T(8,128)(2,1)}, bf16[272,1152]{1,0:T(8,128)(2,1)S(1)}, u32[]{:S(2)}, u32[]{:S(2)}) collective-permute-start(bf16[272,1152]{1,0:T(8,128)(2,1)} %collective-permute-done.1.refs_1_), channel_id=1, source_target_pairs={{32,0},{33,1},{34,2},{35,3},{36,4},{37,5},{38,6},{39,7},{40,8},{41... | collective-permute-start | bytes 1880072 | tf_op jit(solution)/shard_map/ppermute | solution.py:32
  49.1 22.6 %collective-permute-start.15 = (bf16[272,1152]{1,0:T(8,128)(2,1)S(1)}, bf16[272,1152]{1,0:T(8,128)(2,1)S(1)}, u32[]{:S(2)}, u32[]{:S(2)}) collective-permute-start(bf16[272,1152]{1,0:T(8,128)(2,1)S(1)} %collective-permute-done.10.refs_7_), channel_id=1, source_target_pairs={{224,0},{225,1},{226,2},{227,3},{228,4},{229,5},{230,6},{231,7},{2... | collective-permute-start | bytes 1880072 | tf_op jit(solution)/shard_map/ppermute | solution.py:32
  49.8 21.9 %collective-permute-start.16 = (bf16[272,1152]{1,0:T(8,128)(2,1)S(1)}, bf16[272,1152]{1,0:T(8,128)(2,1)S(1)}, u32[]{:S(2)}, u32[]{:S(2)}) collective-permute-start(bf16[272,1152]{1,0:T(8,128)(2,1)S(1)} %collective-permute-done.10.refs_7_), channel_id=1, source_target_pairs={{4,0},{5,1},{6,2},{7,3},{16,4},{17,5},{18,6},{19,7},{12,8},{13,9},... | collective-permute-start | bytes 1880072 | tf_op jit(solution)/shard_map/ppermute | solution.py:32
  50.3 21.4 %collective-permute-start.14 = (bf16[272,1152]{1,0:T(8,128)(2,1)S(1)}, bf16[272,1152]{1,0:T(8,128)(2,1)S(1)}, u32[]{:S(2)}, u32[]{:S(2)}) collective-permute-start(bf16[272,1152]{1,0:T(8,128)(2,1)S(1)} %collective-permute-done.11.refs_5_), channel_id=1, source_target_pairs={{32,0},{33,1},{34,2},{35,3},{36,4},{37,5},{38,6},{39,7},{40,8},{41... | collective-permute-start | bytes 1880072 | tf_op jit(solution)/shard_map/ppermute | solution.py:32
  52.2 19.5 %collective-permute-start.17 = (bf16[272,1152]{1,0:T(8,128)(2,1)S(1)}, bf16[272,1152]{1,0:T(8,128)(2,1)S(1)}, u32[]{:S(2)}, u32[]{:S(2)}) collective-permute-start(bf16[272,1152]{1,0:T(8,128)(2,1)S(1)} %collective-permute-done.12.refs_8_.refs_0_), channel_id=1, source_target_pairs={{3,0},{0,1},{1,2},{2,3},{7,4},{4,5},{5,6},{6,7},{11,8},{8,9},{9,10... | collective-permute-start | bytes 1880072 | tf_op jit(solution)/shard_map/ppermute | solution.py:32
  91.4 9.5 %collective-permute-start.23 = (bf16[32,1152]{1,0:T(8,128)(2,1)S(1)}, bf16[32,1152]{1,0:T(8,128)(2,1)S(1)}, u32[]{:S(2)}, u32[]{:S(2)}) collective-permute-start(bf16[32,1152]{1,0:T(8,128)(2,1)S(1)} %unit.1), channel_id=1, source_target_pairs={{16,0},{17,1},{18,2},{19,3},{20,4},{21,5},{22,6},{23,7},{24,8},{25... | collective-permute-start | bytes 221192 | tf_op jit(solution)/shard_map/ppermute | solution.py:32
  97.4 14.4 %collective-permute-start.22 = (bf16[128,1152]{1,0:T(8,128)(2,1)S(1)}, bf16[128,1152]{1,0:T(8,128)(2,1)S(1)}, u32[]{:S(2)}, u32[]{:S(2)}) collective-permute-start(bf16[128,1152]{1,0:T(8,128)(2,1)S(1)} %pad_maximum_fusion.refs_0_), channel_id=1, source_target_pairs={{4,0},{5,1},{6,2},{7,3},{16,4},{17,5},{18,6},{19,7},{12,8},{13,9},... | collective-permute-start | bytes 884744 | tf_op jit(solution)/shard_map/ppermute | solution.py:32
  99.9 12.1 %collective-permute-start.27 = (bf16[128,1152]{1,0:T(8,128)(2,1)S(1)}, bf16[128,1152]{1,0:T(8,128)(2,1)S(1)}, u32[]{:S(2)}, u32[]{:S(2)}) collective-permute-start(bf16[128,1152]{1,0:T(8,128)(2,1)S(1)} %pad_maximum_fusion.refs_0_), channel_id=1, source_target_pairs={{20,0},{21,1},{22,2},{23,3},{0,4},{1,5},{2,6},{3,7},{28,8},{29,9},... | collective-permute-start | bytes 884744 | tf_op jit(solution)/shard_map/ppermute | solution.py:32
  99.9 21.5 %collective-permute-start.28 = (bf16[128,1152]{1,0:T(8,128)(2,1)S(1)}, bf16[128,1152]{1,0:T(8,128)(2,1)S(1)}, u32[]{:S(2)}, u32[]{:S(2)}) collective-permute-start(bf16[128,1152]{1,0:T(8,128)(2,1)S(1)} %pad_maximum_fusion.refs_0_), channel_id=1, source_target_pairs={{8,0},{9,1},{10,2},{11,3},{12,4},{13,5},{14,6},{15,7},{0,8},{1,9},... | collective-permute-start | bytes 884744 | tf_op jit(solution)/shard_map/ppermute | solution.py:32
  109.4 12.0 %collective-permute-start.30 = (bf16[128,1152]{1,0:T(8,128)(2,1)S(1)}, bf16[128,1152]{1,0:T(8,128)(2,1)S(1)}, u32[]{:S(2)}, u32[]{:S(2)}) collective-permute-start(bf16[128,1152]{1,0:T(8,128)(2,1)S(1)} %constant_dynamic-update-slice_fusion.refs_2_), channel_id=1, source_target_pairs={{8,0},{9,1},{10,2},{11,3},{12,4},{13,5},{14,6},{15,7},{0,8},{1,9},... | collective-permute-start | bytes 884744 | tf_op jit(solution)/shard_map/ppermute | solution.py:32
  111.8 9.6 %collective-permute-start.29 = (bf16[128,1152]{1,0:T(8,128)(2,1)S(1)}, bf16[128,1152]{1,0:T(8,128)(2,1)S(1)}, u32[]{:S(2)}, u32[]{:S(2)}) collective-permute-start(bf16[128,1152]{1,0:T(8,128)(2,1)S(1)} %collective-permute-done.22.refs_1_), channel_id=1, source_target_pairs={{8,0},{9,1},{10,2},{11,3},{12,4},{13,5},{14,6},{15,7},{0,8},{1,9},... | collective-permute-start | bytes 884744 | tf_op jit(solution)/shard_map/ppermute | solution.py:32
  111.9 9.5 %collective-permute-start.31 = (bf16[128,1152]{1,0:T(8,128)(2,1)S(1)}, bf16[128,1152]{1,0:T(8,128)(2,1)S(1)}, u32[]{:S(2)}, u32[]{:S(2)}) collective-permute-start(bf16[128,1152]{1,0:T(8,128)(2,1)S(1)} %collective-permute-done.27.refs_3_), channel_id=1, source_target_pairs={{8,0},{9,1},{10,2},{11,3},{12,4},{13,5},{14,6},{15,7},{0,8},{1,9},... | collective-permute-start | bytes 884744 | tf_op jit(solution)/shard_map/ppermute | solution.py:32
  126.3 9.3 %collective-permute-start.36 = (bf16[32,1152]{1,0:T(8,128)(2,1)S(1)}, bf16[32,1152]{1,0:T(8,128)(2,1)S(1)}, u32[]{:S(2)}, u32[]{:S(2)}) collective-permute-start(bf16[32,1152]{1,0:T(8,128)(2,1)S(1)} %get-tuple-element.56), channel_id=1, source_target_pairs={{160,0},{161,1},{162,2},{163,3},{164,4},{165,5},{166,6},{167,7},{1... | collective-permute-start | bytes 221192 | tf_op jit(solution)/shard_map/ppermute | solution.py:32
  (27 other events, 189.7 us)
